TPU v7x, 256 devices: a whole 4x4x8 slice. The times are simulated.
256 devices in a mesh: section: 4 (over y), orient: 64 (over z, x, core).
Axes of the slice: x: 4, y: 4, z: 8, core: 2. Of those that a mesh axis runs over, the one named last changes fastest.
Arguments:
- patterns: bfloat16 [4, 128, 65536], P('section', None, 'orient'), may hold values from -6 to 6
- detector_gain: float32 [65536], P('orient'), may hold values from 0.1 to 1.9
- background: float32 [65536], P('orient'), may hold values from -6 to 6
- bin_map: int32 [65536], P('orient'), may hold values from 0 to 12287, as said below
- templates: bfloat16 [102400, 12288], P(('section', 'orient')), may hold values from -0.0546875 to 0.0546875
- best_picks: int32 [4, 128], replicated, may hold values from 0 to 102399
Outputs:
- top_scores: float32 [4, 128, 8], P('section')
- refined: float32 [4, 128, 3], P('section', 'orient')
Inputs may be any that keep to these rules, and one draw needn't show every extreme that they name: `bin_map`: each pixel's polar bin r * 192 + a, with r given by the pixel's distance and a by its direction from a beam centre near the middle of the square detector.
All inputs are finite; a program needn't handle non-finite values.
Results may differ from a plain program's by a relative error of at most 0.0065.
Values may be sent and summed in bfloat16 or wider, within the bound.
A program may use at most 256 MiB of HBM per device.

v0:
```python
import jax
import jax.numpy as jnp
from jax import lax
from jax.sharding import PartitionSpec as P

RAD = 64
ANG = 192
TOPK = 8
REACH = 1


EPS = 1e-06
BLOCK_ROWS = 512


def shifted(x, axis, by):
    count = lax.axis_size(axis)
    return lax.ppermute(x, axis, [(i, (i + by) % count) for i in range(count)])


def merged_2(part, axis, combine):
    gathered = lax.all_gather(part, axis)

    def take(source):
        return lax.dynamic_index_in_dim(gathered, source, 0, False)

    return lax.fori_loop(
        1, lax.axis_size(axis), lambda source, state: combine(state, take(source)), take(0)
    )


def bin_block(corrected, bin_map, first, length):
    targets = first + lax.iota(jnp.int32, length)
    onehot = (bin_map[None, :] == targets[:, None]).astype(jnp.bfloat16)
    return lax.dot_general(
        onehot, corrected, (((1,), (1,)), ((), ())), preferred_element_type=jnp.float32
    )


def bin_rows(corrected, bin_map, length):
    blocks = 1
    while length // blocks > BLOCK_ROWS and length % (2 * blocks) == 0:
        blocks = blocks * 2
    height = length // blocks
    starts = height * lax.iota(jnp.int32, blocks)
    stacked = lax.map(lambda begin: bin_block(corrected, bin_map, begin, height), starts)
    return stacked.reshape(length, corrected.shape[0])


def merge_best(first_best, second_best):
    return lax.top_k(jnp.concatenate([first_best, second_best], axis=-1), TOPK)[0]


def score_batch(features, templates, wanted, group_base):
    scores = lax.dot_general(
        features, templates, (((0,), (1,)), ((), ())), preferred_element_type=jnp.float32
    )
    best = lax.top_k(scores, TOPK)[0]
    local = wanted - group_base
    count = templates.shape[0]
    owned = (local >= 0) & (local < count)
    chosen = jnp.take(templates, jnp.clip(local, 0, count - 1), axis=0)
    width = features.shape[1]
    chosen = chosen.reshape(width, RAD, ANG)
    grid = features.T.reshape(width, RAD, ANG)
    columns = []
    for offset in range(-REACH, REACH + 1):
        rolled = jnp.roll(chosen, -offset, axis=2)
        columns.append(jnp.sum(grid.astype(jnp.float32) * rolled.astype(jnp.float32), axis=(1, 2)))
    refined = jnp.where(owned[:, None], jnp.stack(columns, axis=1), 0.0)
    return (best, refined)


def body(patterns, detector_gain, background, bin_map, templates, best_picks):
    sections = lax.axis_size("section")
    orients = lax.axis_size("orient")
    section_index = lax.axis_index("section")
    orient_index = lax.axis_index("orient")
    features_total = RAD * ANG
    corrected = ((patterns[0].astype(jnp.float32) - background) * detector_gain).astype(
        jnp.bfloat16
    )
    whole = lax.psum(bin_rows(corrected, bin_map, features_total), "orient")
    squares = jnp.sum(whole * whole, axis=0)
    features = (whole * lax.rsqrt(squares / features_total + EPS)).astype(jnp.bfloat16)
    group_base = (section_index * orients + orient_index) * templates.shape[0]
    held = features
    running_best = None
    running_refined = None
    for turn in range(sections):
        batch = (section_index + sections - turn) % sections
        wanted = lax.dynamic_index_in_dim(best_picks, batch, 0, keepdims=False)
        best, refined = score_batch(held, templates, wanted, group_base)
        if turn > 0:
            best = merge_best(running_best, best)
            refined = running_refined + refined
        packed = shifted(jnp.concatenate([best, refined], axis=1), "section", 1)
        running_best = packed[:, :TOPK]
        running_refined = packed[:, TOPK:]
        if turn + 1 < sections:
            held = shifted(held, "section", 1)
    merged = merged_2(running_best, "orient", merge_best)
    shares = lax.psum_scatter(running_refined, "orient", scatter_dimension=0, tiled=True)
    return (merged[None], shares[None])


def solution(mesh):
    return jax.shard_map(
        body,
        mesh=mesh,
        in_specs=(
            P("section", None, "orient"),
            P("orient"),
            P("orient"),
            P("orient"),
            P(("section", "orient"), None),
            P(),
        ),
        out_specs=(P("section", None, None), P("section", "orient", None)),
        check_vma=False,
    )
```

profile of v0, /device:TPU:1, one launch (start us, length us, event | category | flops | bytes accessed | tf_op | source)
XLA Modules:
  0.0 811.8 jit_solution(5472753038101455610)
XLA Ops:
  8.3 96.8 %while.25 = (s32[]{:T(128)}, f32[32,384,128]{2,1,0:T(8,128)}, s32[1024]{0:T(1024)}, s32[32]{0:T(128)S(1)}, bf16[128,1024]{1,0:T(8,128)(2,1)S(1)}, /*index=5*/s32[]{:T(128)}) while((s32[]{:T(128)}, f32[32,384,128]{2,1,0:T(8,128)}, s32[1024]{0:T(1024)}, s32[32]{0:T(128)S(1)}, bf16[128,1024]{1,0:T(8,128)(2,1)S(1)}, /*index=5*/s32[]{:T(128)}) %tuple.90), condition=%wide.region_1.2_spmd, body=%wide.region_0.1_spmd.sunk | while | flops 101056896 | bytes 466517 | solution.py:46
  105.1 6.6 copy.74
  112.4 10.4 %gather_fusion = bf16[128,12288]{1,0:T(8,128)(2,1)S(1)} fusion(bf16[400,12288]{1,0:T(8,128)(2,1)} %param.16, s32[1024]{0:T(1024)S(1)} %get-tuple-element.217), kind=kCustom, calls=%fused_computation.clone | custom fusion | bytes 6291968 | tf_op jit(solution)/shard_map/jit(_take)/gather | solution.py:62
  126.5 3.7 copy.50
  130.2 4.2 fusion.34
  134.4 10.6 %gather_fusion.1 = bf16[128,12288]{1,0:T(8,128)(2,1)S(1)} fusion(bf16[400,12288]{1,0:T(8,128)(2,1)} %param.16, s32[1024]{0:T(1024)S(1)} %get-tuple-element.216), kind=kCustom, calls=%fused_computation.1.clone | custom fusion | bytes 6291968 | tf_op jit(solution)/shard_map/jit(_take)/gather | solution.py:62
  148.6 3.7 copy.56
  152.3 4.3 fusion.32
  156.7 10.5 %gather_fusion.2 = bf16[128,12288]{1,0:T(8,128)(2,1)S(1)} fusion(bf16[400,12288]{1,0:T(8,128)(2,1)} %param.16, s32[1024]{0:T(1024)S(1)} %get-tuple-element.215), kind=kCustom, calls=%fused_computation.2.clone | custom fusion | bytes 6291968 | tf_op jit(solution)/shard_map/jit(_take)/gather | solution.py:62
  170.9 3.9 copy.61
  174.8 4.2 fusion.30
  179.1 10.4 %gather_fusion.3 = bf16[128,12288]{1,0:T(8,128)(2,1)S(1)} fusion(bf16[400,12288]{1,0:T(8,128)(2,1)} %param.16, s32[1024]{0:T(1024)S(1)} %get-tuple-element.214), kind=kCustom, calls=%fused_computation.3.clone | custom fusion | bytes 6291968 | tf_op jit(solution)/shard_map/jit(_take)/gather | solution.py:62
  193.2 3.5 copy.66
  196.7 4.1 fusion.28
  201.8 3.3 bitcast_convert_fusion.6
  207.0 3.2 bitcast_convert_fusion.7
  212.2 3.2 bitcast_convert_fusion.5
  216.1 3.2 bitcast_convert_fusion.4
  225.3 6.6 copy.52
  232.0 6.7 copy.51
  244.5 69.9 %all-reduce.3.cloned.1.call-done = f32[12288,128]{0,1:T(8,128)} async-done(((f32[12288,128]{0,1:T(8,128)}), f32[12288,128]{0,1:T(8,128)}) %all-reduce.3.cloned.1.call-update) | async-done | bytes 6291472 | tf_op jit(solution)/shard_map/psum | solution.py:83
  314.4 3.4 multiply_reduce_fusion
  317.9 10.2 %fusion.19 = (f32[128]{0:T(128)}, f32[128]{0:T(128)}, f32[128]{0:T(128)}, bf16[12288,128]{0,1:T(8,128)(2,1)}) fusion(f32[128,12288]{1,0:T(8,128)} %copy.51, f32[128,12288]{1,0:T(8,128)} %copy.52, f32[12288,128]{0,1:T(8,128)} %all-reduce.3.cloned.1.call-done, f32[128]{0:T(128)S(1)} %add_rsqrt_fusion, bf16[128,12288]{1,0:T(8,128)(2,1)S(1)} %copy-done.7, ...), kind=kLoop, calls=%fused_computation.34 | loop fusion | flops 17301120 | bytes 25168000 | tf_op jit(solution)/shard_map/reduce_sum | solution.py:69
  332.4 4.7 fusion.36
  337.1 7.6 top_k.60
  349.4 47.6 %collective-permute-done.1 = bf16[12288,128]{0,1:T(8,128)(2,1)} collective-permute-done((bf16[12288,128]{0,1:T(8,128)(2,1)}, bf16[12288,128]{0,1:T(8,128)(2,1)}, u32[]{:S(2)}, u32[]{:S(2)}) %collective-permute-start.1) | collective-permute-done | bytes 3145760 | tf_op jit(solution)/shard_map/ppermute | solution.py:18
  397.0 3.1 bitcast_convert_fusion.1
  400.1 6.5 copy.57
  406.6 6.6 copy.58
  414.4 6.6 fusion.37
  421.0 7.7 top_k.62
  432.7 6.8 fusion.16
  443.6 7.0 copy.62
  450.6 6.6 copy.63
  457.2 7.9 collective-permute-done.2
  465.6 6.6 fusion.38
  472.2 7.6 top_k.70
  482.6 6.7 fusion.13
  490.0 4.4 bitcast_convert_fusion
  494.4 6.6 copy.67
  501.0 6.6 copy.68
  507.6 42.1 %collective-permute-done.4 = f32[128,11]{0,1:T(8,128)S(1)} collective-permute-done((f32[128,11]{0,1:T(8,128)S(1)}, f32[128,11]{0,1:T(8,128)S(1)}, u32[]{:S(2)}, u32[]{:S(2)}) %collective-permute-start.4) | collective-permute-done | bytes 5664 | tf_op jit(solution)/shard_map/ppermute | solution.py:18
  550.4 6.6 fusion.39
  557.0 7.6 top_k.74
  567.2 6.7 fusion.10
  578.3 55.7 %all-gather = f32[8192,8]{0,1:T(8,128)S(1)} all-gather(f32[128,8]{0,1:T(8,128)S(1)} %slice.147), channel_id=2, replica_groups=mesh['section'=4,'orient'=64] {'orient'}, dimensions={0}, use_global_device_ids=true | all-gather | bytes 266240 | tf_op jit(solution)/shard_map/all_gather | solution.py:22
  634.0 46.4 %while.26 = (s32[]{:T(128)}, f32[128,8]{0,1:T(8,128)S(1)}, f32[64,128,8]{1,2,0:T(8,128)S(1)}, s32[]{:T(128)}, s32[]{:T(128)}, /*index=5*/s32[]{:T(128)}) while((s32[]{:T(128)}, f32[128,8]{0,1:T(8,128)S(1)}, f32[64,128,8]{1,2,0:T(8,128)S(1)}, s32[]{:T(128)}, s32[]{:T(128)}, /*index=5*/s32[]{:T(128)}) %tuple.98), condition=%wide.region_25.27_spmd, body=%wide.region_23.26_spmd.sunk | while | flops 24581 | bytes 73843 | solution.py:27
  680.5 123.6 %all-reduce = f32[128,3]{0,1:T(4,128)S(1)} all-reduce(f32[128,3]{0,1:T(4,128)S(1)} %slice.149), channel_id=3, replica_groups=mesh['section'=4,'orient'=64] {'orient'}, use_global_device_ids=true, to_apply=%region_26.28.clone | all-reduce | flops 384 | bytes 3072
  (566 shorter events, 206.9 us)
Async XLA Ops:
  7.2 307.2 %all-reduce.3.cloned.1.call-start = ((), (), s32[]{:S(2)}) async-start(), calls=%async_computation | async-start | bytes 12582912 | tf_op jit(solution)/shard_map/psum | solution.py:83
  111.6 0.7 copy-start.23
  112.4 32.6 %copy-start.26 = (pred[128]{0:T(512)(128)(4,1)}, pred[128]{0:T(512)(128)(4,1)S(1)}, u32[]{:S(2)}) copy-start(pred[128]{0:T(512)(128)(4,1)S(1)} %get-tuple-element.208) | copy-start | bytes 388
  112.4 54.9 %copy-start.25 = (pred[128]{0:T(512)(128)(4,1)}, pred[128]{0:T(512)(128)(4,1)S(1)}, u32[]{:S(2)}) copy-start(pred[128]{0:T(512)(128)(4,1)S(1)} %get-tuple-element.210) | copy-start | bytes 388
  112.4 77.1 %copy-start.24 = (pred[128]{0:T(512)(128)(4,1)}, pred[128]{0:T(512)(128)(4,1)S(1)}, u32[]{:S(2)}) copy-start(pred[128]{0:T(512)(128)(4,1)S(1)} %get-tuple-element.179) | copy-start | bytes 388
  122.8 1.7 copy-start.6
  145.0 1.6 copy-start.4
  167.2 1.6 copy-start.2
  189.5 1.7 copy-start
  196.7 4.8 copy-start.13
  201.8 3.7 copy-start.10
  207.0 3.7 copy-start.14
  212.2 3.6 copy-start.11
  216.1 3.6 copy-start.16
  219.8 3.0 copy-start.15
  232.0 6.7 copy-start.12
  238.7 3.0 copy-start.18
  244.5 73.3 %copy-start.7 = (bf16[128,12288]{1,0:T(8,128)(2,1)S(1)}, bf16[128,12288]{1,0:T(8,128)(2,1)}, u32[]{:S(2)}) copy-start(bf16[128,12288]{1,0:T(8,128)(2,1)} %copy-done.6) | copy-start | bytes 9437188
  314.4 17.9 %slice-start = ((s8[9830400]{0:T(1024)(128)(4,1)}), s8[4194304]{0:T(1024)(128)(4,1)S(1)}, s32[]{:S(2)}) async-start(s8[9830400]{0:T(1024)(128)(4,1)} %bitcast.134), calls=%async_computation.1 | async-start | bytes 8388608
  317.8 11.4 %copy-start.17 = (bf16[128,64,192]{0,2,1:T(8,128)(2,1)S(1)}, bf16[128,64,192]{0,2,1:T(8,128)(2,1)}, u32[]{:S(2)}) copy-start(bf16[128,64,192]{0,2,1:T(8,128)(2,1)} %pad_maximum_fusion.6) | copy-start | bytes 9437188
  317.8 14.5 %slice-start.1 = ((s8[9830400]{0:T(1024)(128)(4,1)}), s8[4194304]{0:T(1024)(128)(4,1)S(1)}, s32[]{:S(2)}) async-start(s8[9830400]{0:T(1024)(128)(4,1)} %bitcast.134), calls=%async_computation.2 | async-start | bytes 8388608
  317.9 14.5 %slice-start.2 = ((s8[9830400]{0:T(1024)(128)(4,1)}), s8[1441792]{0:T(1024)(128)(4,1)S(1)}, s32[]{:S(2)}) async-start(s8[9830400]{0:T(1024)(128)(4,1)} %bitcast.134), calls=%async_computation.3 | async-start | bytes 2883584
  328.1 68.9 %collective-permute-start.1 = (bf16[12288,128]{0,1:T(8,128)(2,1)}, bf16[12288,128]{0,1:T(8,128)(2,1)}, u32[]{:S(2)}, u32[]{:S(2)}) collective-permute-start(bf16[12288,128]{0,1:T(8,128)(2,1)} %get-tuple-element.185), channel_id=1, source_target_pairs={{0,64},{64,128},{128,192},{192,0},{1,65},{65,129},{129,193},{193,1... | collective-permute-start | bytes 9437192 | tf_op jit(solution)/shard_map/ppermute | solution.py:18
  332.4 64.6 %copy-start.9 = (bf16[128,64,192]{0,2,1:T(8,128)(2,1)S(1)}, bf16[128,64,192]{0,2,1:T(8,128)(2,1)}, u32[]{:S(2)}) copy-start(bf16[128,64,192]{0,2,1:T(8,128)(2,1)} %pad_maximum_fusion.7) | copy-start | bytes 9437188
  348.1 65.1 %collective-permute-start = (f32[128,11]{0,1:T(8,128)S(1)}, f32[128,11]{0,1:T(8,128)S(1)}, u32[]{:S(2)}, u32[]{:S(2)}) collective-permute-start(f32[128,11]{0,1:T(8,128)S(1)} %pad_maximum_fusion.9), channel_id=1, source_target_pairs={{0,64},{64,128},{128,192},{192,0},{1,65},{65,129},{129,193},{193,1... | collective-permute-start | bytes 16904 | tf_op jit(solution)/shard_map/ppermute | solution.py:18
  397.0 68.7 %collective-permute-start.3 = (bf16[12288,128]{0,1:T(8,128)(2,1)}, bf16[12288,128]{0,1:T(8,128)(2,1)}, u32[]{:S(2)}, u32[]{:S(2)}) collective-permute-start(bf16[12288,128]{0,1:T(8,128)(2,1)} %collective-permute-done.1), channel_id=1, source_target_pairs={{0,64},{64,128},{128,192},{192,0},{1,65},{65,129},{129,193},{193,1... | collective-permute-start | bytes 9437192 | tf_op jit(solution)/shard_map/ppermute | solution.py:18
  413.2 0.6 copy-start.27
  414.4 18.4 %copy-start.5 = (bf16[128,12288]{1,0:T(8,128)(2,1)S(1)}, bf16[128,12288]{1,0:T(8,128)(2,1)}, u32[]{:S(2)}) copy-start(bf16[128,12288]{1,0:T(8,128)(2,1)} %copy-done.4) | copy-start | bytes 9437188
  432.7 6.8 copy-start.31
  432.7 8.8 %copy-start.8 = (bf16[128,64,191]{0,2,1:T(8,128)(2,1)S(1)}, bf16[128,64,191]{0,2,1:T(8,128)(2,1)}, u32[]{:S(2)}) copy-start(bf16[128,64,191]{0,2,1:T(8,128)(2,1)} %get-tuple-element.188) | copy-start | bytes 9388036
  432.7 8.8 %copy-start.20 = (bf16[128,64,1]{0,2,1:T(2,128)(2,1)S(1)}, bf16[128,64,1]{0,2,1:T(2,128)(2,1)}, u32[]{:S(2)}) copy-start(bf16[128,64,1]{0,2,1:T(2,128)(2,1)} %get-tuple-element.190) | copy-start | bytes 49156
  440.3 24.8 %collective-permute-start.2 = (f32[128,11]{0,1:T(8,128)S(1)}, f32[128,11]{0,1:T(8,128)S(1)}, u32[]{:S(2)}, u32[]{:S(2)}) collective-permute-start(f32[128,11]{0,1:T(8,128)S(1)} %pad_maximum_fusion.11), channel_id=1, source_target_pairs={{0,64},{64,128},{128,192},{192,0},{1,65},{65,129},{129,193},{193,1... | collective-permute-start | bytes 16904 | tf_op jit(solution)/shard_map/ppermute | solution.py:18
  465.0 0.6 copy-start.21
  465.6 16.9 %copy-start.3 = (bf16[128,12288]{1,0:T(8,128)(2,1)S(1)}, bf16[128,12288]{1,0:T(8,128)(2,1)}, u32[]{:S(2)}) copy-start(bf16[128,12288]{1,0:T(8,128)(2,1)} %copy-done.2) | copy-start | bytes 9437188
  482.5 6.8 copy-start.22
  482.5 6.8 copy-start.30
  482.5 6.8 slice-start.3
  482.5 67.9 %collective-permute-start.5 = (bf16[12288,128]{0,1:T(8,128)(2,1)}, bf16[12288,128]{0,1:T(8,128)(2,1)}, u32[]{:S(2)}, u32[]{:S(2)}) collective-permute-start(bf16[12288,128]{0,1:T(8,128)(2,1)} %collective-permute-done.3), channel_id=1, source_target_pairs={{0,64},{64,128},{128,192},{192,0},{1,65},{65,129},{129,193},{193,1... | collective-permute-start | bytes 9437192 | tf_op jit(solution)/shard_map/ppermute | solution.py:18
  490.0 59.7 %collective-permute-start.4 = (f32[128,11]{0,1:T(8,128)S(1)}, f32[128,11]{0,1:T(8,128)S(1)}, u32[]{:S(2)}, u32[]{:S(2)}) collective-permute-start(f32[128,11]{0,1:T(8,128)S(1)} %pad_maximum_fusion.13), channel_id=1, source_target_pairs={{0,64},{64,128},{128,192},{192,0},{1,65},{65,129},{129,193},{193,1... | collective-permute-start | bytes 16904 | tf_op jit(solution)/shard_map/ppermute | solution.py:18
  549.8 0.6 copy-start.28
  550.4 16.8 %copy-start.1 = (bf16[128,12288]{1,0:T(8,128)(2,1)S(1)}, bf16[128,12288]{1,0:T(8,128)(2,1)}, u32[]{:S(2)}) copy-start(bf16[128,12288]{1,0:T(8,128)(2,1)} %copy-done) | copy-start | bytes 9437188
  567.2 6.7 copy-start.29
  567.2 7.5 copy-start.32
  574.5 3.8 collective-permute-start.6
  680.5 124.3 %copy-start.19 = (f32[128,8]{0,1:T(8,128)}, f32[128,8]{0,1:T(8,128)S(1)}, u32[]{:S(2)}) copy-start(f32[128,8]{0,1:T(8,128)S(1)} %get-tuple-element.142) | copy-start | bytes 12292
Sparse Core Ops, SparseCore 0:
  111.8 202.5 all-reduce.2
where the time goes:
time: 821 us; the launch traced here: 812 us
  other arithmetic  186 us (23%)
  blocking collectives  179 us (22%)
  local copies, waits for them, and re-layouts  175 us (21%)
  waiting for transfers between devices  170 us (21%)
  matrix products  81.6 us (10%)
  between operations  15.5 us (2%)
    unnamed x1, blocking collectives  124 us
    ppermute x7, waiting for transfers between devices, shifted(): return lax.ppermute(x, axis, [(i, (i + by) % count) for i in range(count)])  100 us
    psum x1, waiting for transfers between devices, body(): whole = lax.psum(bin_rows(corrected, bin_map, features_total), 'orient')  69.9 us
    dot_general x32, matrix products, bin_block(): lax.dot_general(onehot, corrected, (((1,), (1,)), ((), ())), preferred_el...  57.2 us
    all_gather x1, blocking collectives, merged_2(): gathered = lax.all_gather(part, axis)  55.7 us
    convert_element_type x8, local copies, waits for them, and re-layouts, score_batch(): rolled.astype(jnp.float32)  53.2 us
    top_k x66, other arithmetic, merge_best(): lax.top_k(jnp.concatenate([first_best, second_best], axis=-1), TOPK)[0]  47.6 us
    gather x4, local copies, waits for them, and re-layouts, score_batch(): chosen = jnp.take(templates, jnp.clip(local, 0, count - 1), axis=0)  41.8 us
  transfers between devices with their start and end apart: 8, of which 5 were waited for; matrix products, arithmetic and copies ran while one was open for 28% of the time, Pallas kernels for 0%

commit v1 on v0

v1 whole, which is shorter than its diff:
```python
import functools

import jax
import jax.numpy as jnp
from jax import lax
from jax.experimental import pallas as pl
from jax.experimental.pallas import tpu as pltpu
from jax.sharding import PartitionSpec as P

RAD = 64
ANG = 192
TOPK = 8
REACH = 1


EPS = 1e-06
BIN_BLOCK = 1024


def bin_kernel(pat_ref, bg_ref, gain_ref, map_ref, out_ref, corr_ref):
    step = pl.program_id(0)

    @pl.when(step == 0)
    def _():
        corr_ref[...] = (
            (pat_ref[...].astype(jnp.float32) - bg_ref[...]) * gain_ref[...]
        ).astype(jnp.bfloat16)

    height, width = out_ref.shape[0], map_ref.shape[1]
    targets = step * height + lax.broadcasted_iota(jnp.int32, (height, width), 0)
    onehot = (map_ref[...] == targets).astype(jnp.bfloat16)
    out_ref[...] = lax.dot_general(
        onehot, corr_ref[...], (((1,), (1,)), ((), ())), preferred_element_type=jnp.float32
    )


def bin_pixels(frames, background, gain, bin_map, total):
    rows, width = frames.shape
    height = min(BIN_BLOCK, total)
    full = lambda step: (0, 0)
    return pl.pallas_call(
        bin_kernel,
        grid=(total // height,),
        in_specs=[
            pl.BlockSpec((rows, width), full),
            pl.BlockSpec((1, width), full),
            pl.BlockSpec((1, width), full),
            pl.BlockSpec((1, width), full),
        ],
        out_specs=pl.BlockSpec((height, rows), lambda step: (step, 0)),
        out_shape=jax.ShapeDtypeStruct((total, rows), jnp.float32),
        scratch_shapes=[pltpu.VMEM((rows, width), jnp.bfloat16)],
        cost_estimate=pl.CostEstimate(
            flops=2 * total * width * rows, transcendentals=0,
            bytes_accessed=rows * width * 2 + total * rows * 4,
        ),
    )(frames, background[None, :], gain[None, :], bin_map[None, :])


def merge_packed(stack, axis):
    best = jnp.moveaxis(stack[..., :TOPK], axis, -2)
    best = best.reshape(best.shape[:-2] + (best.shape[-2] * TOPK,))
    best = lax.top_k(best, TOPK)[0]
    refined = jnp.sum(stack[..., TOPK:], axis=axis)
    return jnp.concatenate([best, refined], axis=-1)


def body(patterns, detector_gain, background, bin_map, templates, best_picks):
    sections = lax.axis_size("section")
    orients = lax.axis_size("orient")
    section_index = lax.axis_index("section")
    orient_index = lax.axis_index("orient")
    features_total = RAD * ANG
    batches, patterns_per = best_picks.shape
    count = templates.shape[0]

    bins = bin_pixels(patterns[0], background, detector_gain, bin_map, features_total)
    part = lax.psum_scatter(bins, "orient", scatter_dimension=0, tiled=True)
    gathered = lax.all_gather(
        part.astype(jnp.bfloat16), ("section", "orient"), axis=0, tiled=True
    ).reshape(batches, features_total, patterns_per)

    wide = gathered.astype(jnp.float32)
    squares = jnp.sum(wide * wide, axis=1)
    scale = lax.rsqrt(squares / features_total + EPS)

    rings = gathered.reshape(batches, RAD, ANG, patterns_per)
    shifted = [jnp.roll(rings, offset, axis=2) for offset in range(-REACH, REACH + 1)]
    stacked = jnp.stack(shifted, axis=0).reshape(
        2 * REACH + 1, batches, features_total, patterns_per
    )
    raw = lax.dot_general(
        stacked, templates, (((2,), (1,)), ((), ())), preferred_element_type=jnp.float32
    )
    scores = raw[REACH] * scale[:, :, None]
    best = lax.top_k(scores, TOPK)[0]

    group_base = (section_index * orients + orient_index) * count
    local = best_picks - group_base
    owned = local[:, :, None] == lax.broadcasted_iota(jnp.int32, (batches, patterns_per, count), 2)
    picked = jnp.sum(jnp.where(owned[None], raw, 0.0), axis=3) * scale[None]
    packed = jnp.concatenate([best, jnp.moveaxis(picked, 0, -1)], axis=-1)

    mine = lax.all_to_all(packed, "section", 0, 0, tiled=True)
    merged = merge_packed(mine, 0)
    everyone = lax.all_gather(merged, "orient", axis=0)
    final = merge_packed(everyone, 0)
    share = patterns_per // orients
    rows = lax.dynamic_slice_in_dim(final[:, TOPK:], orient_index * share, share, axis=0)
    return (final[None, :, :TOPK], rows[None])


def solution(mesh):
    return jax.shard_map(
        body,
        mesh=mesh,
        in_specs=(
            P("section", None, "orient"),
            P("orient"),
            P("orient"),
            P("orient"),
            P(("section", "orient"), None),
            P(),
        ),
        out_specs=(P("section", None, None), P("section", "orient", None)),
        check_vma=False,
    )
```

time: 821 us -> 481 us (0.59); the launches traced: 812 us -> 481 us
  local copies, waits for them, and re-layouts: 175 us -> 23.5 us
  blocking collectives: 179 us -> 44.8 us
  waiting for transfers between devices: 170 us -> 278 us
  other arithmetic: 186 us -> 78.1 us
  matrix products: 81.6 us -> 27.6 us
  Pallas kernels: 0 us -> 10.9 us
    reduce_scatter x0 -> x1, waiting for transfers between devices: none -> 146 us  [body(): part = lax.psum_scatter(bins, 'orient', scatter_dimension=0, tiled=True)]
    all_gather x0 -> x1, waiting for transfers between devices: none -> 128 us  [body(): lax.all_gather(part.astype(jnp.bfloat16), ('section', 'orient'), axis=0,...]
    unnamed x1 -> x0, blocking collectives: 124 us -> none
    ppermute x7 -> x0, waiting for transfers between devices: 100 us -> none  [shifted(): return lax.ppermute(x, axis, [(i, (i + by) % count) for i in range(count)])]
    psum x1 -> x0, waiting for transfers between devices: 69.9 us -> none  [body(): whole = lax.psum(bin_rows(corrected, bin_map, features_total), 'orient')]
    convert_element_type x8 -> x0, local copies, waits for them, and re-layouts: 53.2 us -> none  [score_batch(): rolled.astype(jnp.float32)]
    gather x4 -> x0, local copies, waits for them, and re-layouts: 41.8 us -> none  [score_batch(): chosen = jnp.take(templates, jnp.clip(local, 0, count - 1), axis=0)]
    top_k x70 -> x3, other arithmetic: 78.1 us -> 37 us  [the longest x1 28.4 us: body(): best = lax.top_k(scores, TOPK)[0]]
  transfers between devices with their start and end apart: 8 -> 3, of which waited for: 5 -> 3; matrix products, arithmetic and copies ran while one was open for 28% -> 0% of each run, Pallas kernels for 0% -> 0%
where the time goes in v1:
time: 481 us
  waiting for transfers between devices  278 us (58%)
  other arithmetic  78.1 us (16%)
  blocking collectives  44.8 us (9%)
  matrix products  27.6 us (6%)
  local copies, waits for them, and re-layouts  23.5 us (5%)
  between operations  14.2 us (3%)
  Pallas kernels  10.9 us (2%)
    reduce_scatter x1, waiting for transfers between devices, body(): part = lax.psum_scatter(bins, 'orient', scatter_dimension=0, tiled=True)  146 us
    all_gather x1, waiting for transfers between devices, body(): lax.all_gather(part.astype(jnp.bfloat16), ('section', 'orient'), axis=0,...  128 us
    all_gather x1, blocking collectives, body(): everyone = lax.all_gather(merged, 'orient', axis=0)  44.8 us
    top_k x1, other arithmetic, body(): best = lax.top_k(scores, TOPK)[0]  28.4 us
    dot_general x1, matrix products, body(): lax.dot_general(stacked, templates, (((2,), (1,)), ((), ())), preferred_e...  27.6 us
    slice x2, local copies, waits for them, and re-layouts, body(): jnp.roll(rings, offset, axis=2)  20.3 us
    concatenate x1, other arithmetic, body(): jnp.roll(rings, offset, axis=2)  19.6 us
    pallas_call x1, Pallas kernels, bin_pixels(): pl.pallas_call(bin_kernel, grid=(total // height,), in_specs=[pl.BlockSpe...  10.9 us
  transfers between devices with their start and end apart: 3, of which 3 were waited for; matrix products, arithmetic and copies ran while one was open for 0% of the time, Pallas kernels for 0%

profile of v1, /device:TPU:1, one launch (start us, length us, event | category | flops | bytes accessed | tf_op | source)
XLA Modules:
  0.0 481.1 jit_solution(17263069718596350543)
XLA Ops:
  7.2 0.0 copy-start.1
  7.2 0.0 reduce-scatter.2.cloned.1.call-start
  7.2 10.9 %shard_map.77 = f32[12288,128]{1,0:T(8,128)} custom-call(bf16[128,1024]{1,0:T(8,128)(2,1)} %bitcast.50, f32[1,1024]{1,0:T(1,128)} %bitcast.51, f32[1,1024]{1,0:T(1,128)} %bitcast.52, s32[1,1024]{1,0:T(1,128)} %bitcast.53), custom_call_target="tpu_custom_call" | custom-call | flops 3221225472 | bytes 6553600 | tf_op jit(solution)/shard_map/pallas_call | solution.py:41
  18.1 0.0 reduce-scatter.2.cloned.1.call-update
  18.1 0.0 all-gather.3.cloned.1.call-start
  18.2 145.9 %reduce-scatter.2.cloned.1.call-done = f32[192,128]{1,0:T(8,128)} async-done(((f32[12288,128]{1,0:T(8,128)}), f32[192,128]{1,0:T(8,128)}) %reduce-scatter.2.cloned.1.call-update) | async-done | bytes 98320 | tf_op jit(solution)/shard_map/reduce_scatter | solution.py:78
  164.1 1.5 convert_element_type.7
  165.6 0.0 all-gather.3.cloned.1.call-update
  165.7 0.0 copy-done.1
  165.7 0.1 iota_compare_fusion
  165.8 127.8 %all-gather.3.cloned.1.call-done = bf16[49152,128]{1,0:T(8,128)(2,1)} async-done(((bf16[192,128]{1,0:T(8,128)(2,1)}), bf16[49152,128]{1,0:T(8,128)(2,1)}) %all-gather.3.cloned.1.call-update) | async-done | bytes 12582928 | tf_op jit(solution)/shard_map/all_gather | solution.py:79
  293.6 0.0 copy-start
  293.6 20.1 %fusion.9 = (bf16[4,64,191,128]{3,2,1,0:T(8,128)(2,1)}, bf16[4,64,191,128]{3,2,1,0:T(8,128)(2,1)}) fusion(bf16[4,64,192,128]{3,2,1,0:T(8,128)(2,1)} %bitcast.40), kind=kLoop, calls=%fused_computation.27 | loop fusion | bytes 50069504 | tf_op jit(solution)/shard_map/jit(_roll_static)/slice | solution.py:88
  313.7 0.0 copy-done
  313.7 0.2 fusion.10
  313.9 8.5 %convert_multiply_fusion = f32[49152,128]{1,0:T(8,128)} fusion(bf16[49152,128]{1,0:T(8,128)(2,1)S(1)} %copy-done), kind=kLoop, calls=%fused_computation.6 | loop fusion | flops 12582912 | bytes 37748736 | tf_op jit(solution)/shard_map/mul | solution.py:84
  322.4 10.0 %reduce_sum.36 = f32[4,128]{1,0:T(4,128)S(1)} reduce(f32[4,12288,128]{2,1,0:T(8,128)} %bitcast.43, f32[]{:T(128)} %constant.36.clone.1), dimensions={1}, to_apply=%region_1.0 | reduce | flops 6290944 | bytes 25167876 | tf_op jit(solution)/shard_map/reduce_sum | solution.py:84
  332.5 19.6 %pad_maximum_fusion = (bf16[4,64,192,128]{3,2,1,0:T(8,128)(2,1)S(1)}, bf16[4,64,192,128]{3,2,1,0:T(8,128)(2,1)}) fusion(bf16[4,64,1,128]{3,2,1,0:T(2,128)(2,1)S(1)} %get-tuple-element.23, bf16[4,64,191,128]{3,2,1,0:T(8,128)(2,1)} %get-tuple-element.21, bf16[4,64,191,128]{3,2,1,0:T(8,128)(2,1)} %get-tuple-element.22, ...), kind=kLoop, calls=%fused_computation.7 | loop fusion | flops 50331648 | bytes 50331648 | tf_op jit(solution)/shard_map/jit(_roll_static)/concatenate | solution.py:88
  352.0 27.6 %select_reduce_fusion = (f32[3,4,128]{2,1,0:T(4,128)S(1)}, f32[3,4,128,400]{2,3,1,0:T(8,128)}) fusion(pred[4,128,400]{1,2,0:T(8,128)(4,1)S(1)} %iota_compare_fusion, bf16[1,4,12288,128]{3,2,1,0:T(8,128)(2,1)} %bitcast.45, bf16[1,4,12288,128]{3,2,1,0:T(8,128)(2,1)} %bitcast.41, bf16[1,4,12288,128]{3,2,1,0:T(8,128)(2,1)S(1)} %bitcast.44, ...), kind=kOutput, calls=%fused_computation.10 | convolution fusion | flops 15213967360 | bytes 50247680 | tf_op jit(solution)/shard_map/dot_general | solution.py:92
  379.6 1.2 fusion.7
  380.8 0.1 iota.16.clone
  380.8 28.4 %top_k.23 = (f32[4,128,400]{1,2,0:T(8,128)S(1)}, s32[4,128,400]{1,2,0:T(8,128)}) sort(f32[4,128,400]{1,2,0:T(8,128)S(1)} %fusion.7, s32[4,128,400]{1,2,0:T(8,128)S(1)} %iota.16.clone), dimensions={2}, to_apply=%region_2.3 | sort | flops 3686400 | bytes 3276800 | tf_op jit(solution)/shard_map/top_k | solution.py:96
  409.2 0.3 copy.34
  409.6 0.1 copy.23
  409.8 0.1 pad_maximum_fusion.2
  409.9 0.7 copy.24
  410.7 4.0 all-to-all-start
  414.6 4.3 all-to-all-done
  418.9 0.8 top_k.25
  419.8 44.8 %all-gather = f32[8192,11]{0,1:T(8,128)S(1)} all-gather(f32[128,11]{0,1:T(8,128)S(1)} %pad_maximum_fusion.3), channel_id=2, replica_groups=mesh['section'=4,'orient'=64] {'orient'}, dimensions={0}, use_global_device_ids=true | all-gather | bytes 366080 | tf_op jit(solution)/shard_map/all_gather | solution.py:106
  464.6 0.1 copy.42
  464.8 0.2 copy.44
  465.0 7.8 %top_k.27 = (f32[128,512]{0,1:T(8,128)S(1)}, s32[128,512]{0,1:T(8,128)}) sort(f32[128,512]{0,1:T(8,128)S(1)} %bitcast.48, s32[128,512]{0,1:T(8,128)S(1)} %iota.19.clone), dimensions={1}, to_apply=%region_6.7 | sort | flops 1048576 | bytes 1048576 | tf_op jit(solution)/shard_map/top_k | solution.py:63
  472.8 0.1 copy.38
  472.9 0.7 copy.30
  473.6 0.1 constant_dynamic-slice_fusion
  473.6 0.7 copy.29
  (14 shorter events, 0.2 us)
Async XLA Ops:
  7.2 158.5 %copy-start.1 = (s32[4,128]{1,0:T(4,128)S(1)}, s32[4,128]{1,0:T(4,128)}, u32[]{:S(2)}) copy-start(s32[4,128]{1,0:T(4,128)} %param.11) | copy-start | bytes 6148
  7.2 157.0 %reduce-scatter.2.cloned.1.call-start = ((), (), s32[]{:S(2)}) async-start(), calls=%async_computation.2 | async-start | bytes 6389760 | tf_op jit(solution)/shard_map/reduce_scatter | solution.py:78
  18.1 275.5 %all-gather.3.cloned.1.call-start = ((), (), s32[]{:S(2)}) async-start(), calls=%async_computation.3 | async-start | bytes 12632064 | tf_op jit(solution)/shard_map/all_gather | solution.py:79
  293.6 20.1 %copy-start = (bf16[49152,128]{1,0:T(8,128)(2,1)S(1)}, bf16[49152,128]{1,0:T(8,128)(2,1)}, u32[]{:S(2)}) copy-start(bf16[49152,128]{1,0:T(8,128)(2,1)} %all-gather.3.cloned.1.call-done) | copy-start | bytes 37748740
  410.7 8.3 %all-to-all-start = ((f32[4,128,11]{1,2,0:T(8,128)}), f32[4,128,11]{1,2,0:T(8,128)S(1)}, u32[]{:S(2)}, u32[]{:S(2)}) async-start(f32[4,128,11]{1,2,0:T(8,128)} %copy.24), calls=%async_computation.1 | async-start | bytes 65536 | tf_op jit(solution)/shard_map/all_to_all | solution.py:104
Sparse Core Ops, SparseCore 0:
  18.3 145.8 reduce-scatter.1
  168.6 124.9 all-gather.2

commit v2 on v1

--- a/solution.py
+++ b/solution.py
@@ -57,10 +57,23 @@
     )(frames, background[None, :], gain[None, :], bin_map[None, :])
 
 
+def top_values(values):
+    width = values.shape[-1]
+    place = lax.broadcasted_iota(jnp.int32, values.shape, values.ndim - 1)
+    found = []
+    for rank in range(TOPK):
+        largest = jnp.max(values, axis=-1, keepdims=True)
+        found.append(largest)
+        if rank + 1 < TOPK:
+            first = jnp.min(jnp.where(values == largest, place, width), axis=-1, keepdims=True)
+            values = jnp.where(place == first, -jnp.inf, values)
+    return jnp.concatenate(found, axis=-1)
+
+
 def merge_packed(stack, axis):
     best = jnp.moveaxis(stack[..., :TOPK], axis, -2)
     best = best.reshape(best.shape[:-2] + (best.shape[-2] * TOPK,))
-    best = lax.top_k(best, TOPK)[0]
+    best = top_values(best)
     refined = jnp.sum(stack[..., TOPK:], axis=axis)
     return jnp.concatenate([best, refined], axis=-1)
 
@@ -75,31 +88,30 @@
     count = templates.shape[0]
 
     bins = bin_pixels(patterns[0], background, detector_gain, bin_map, features_total)
-    part = lax.psum_scatter(bins, "orient", scatter_dimension=0, tiled=True)
+    part = lax.psum_scatter(bins.astype(jnp.bfloat16), "orient", scatter_dimension=0, tiled=True)
     gathered = lax.all_gather(
-        part.astype(jnp.bfloat16), ("section", "orient"), axis=0, tiled=True
+        part, ("section", "orient"), axis=0, tiled=True
     ).reshape(batches, features_total, patterns_per)
 
-    wide = gathered.astype(jnp.float32)
-    squares = jnp.sum(wide * wide, axis=1)
+    squares = jnp.einsum(
+        "mfp,mfp->mp", gathered, gathered, preferred_element_type=jnp.float32
+    )
     scale = lax.rsqrt(squares / features_total + EPS)
 
-    rings = gathered.reshape(batches, RAD, ANG, patterns_per)
-    shifted = [jnp.roll(rings, offset, axis=2) for offset in range(-REACH, REACH + 1)]
-    stacked = jnp.stack(shifted, axis=0).reshape(
-        2 * REACH + 1, batches, features_total, patterns_per
-    )
+    slab = templates.reshape(count, RAD, ANG)
+    turned = [jnp.roll(slab, -offset, axis=2) for offset in range(-REACH, REACH + 1)]
+    rotated = jnp.concatenate(turned, axis=0).reshape((2 * REACH + 1) * count, features_total)
     raw = lax.dot_general(
-        stacked, templates, (((2,), (1,)), ((), ())), preferred_element_type=jnp.float32
-    )
-    scores = raw[REACH] * scale[:, :, None]
-    best = lax.top_k(scores, TOPK)[0]
+        gathered, rotated, (((1,), (1,)), ((), ())), preferred_element_type=jnp.float32
+    ).reshape(batches, patterns_per, 2 * REACH + 1, count)
+    scores = raw[:, :, REACH] * scale[:, :, None]
+    best = top_values(scores)
 
     group_base = (section_index * orients + orient_index) * count
     local = best_picks - group_base
     owned = local[:, :, None] == lax.broadcasted_iota(jnp.int32, (batches, patterns_per, count), 2)
-    picked = jnp.sum(jnp.where(owned[None], raw, 0.0), axis=3) * scale[None]
-    packed = jnp.concatenate([best, jnp.moveaxis(picked, 0, -1)], axis=-1)
+    picked = jnp.sum(jnp.where(owned[:, :, None], raw, 0.0), axis=3) * scale[:, :, None]
+    packed = jnp.concatenate([best, picked], axis=-1)
 
     mine = lax.all_to_all(packed, "section", 0, 0, tiled=True)
     merged = merge_packed(mine, 0)

time: 481 us -> 404 us (0.84)
  waiting for transfers between devices: 278 us -> 145 us
  local copies, waits for them, and re-layouts: 23.5 us -> 87.7 us
  other arithmetic: 78.1 us -> 68.3 us
  matrix products: 27.6 us -> 21.3 us
  blocking collectives: 44.8 us -> 50.3 us
    all_gather x1, waiting for transfers between devices: 128 us -> 0.02 us  [body(): lax.all_gather(part, ('section', 'orient'), axis=0, tiled=True)]
    concatenate x1 -> x5, local copies, waits for them, and re-layouts: 0.72 us -> 41.7 us  [the longest x2 39.8 us: body(): jnp.concatenate(turned, axis=0)]
    top_k x3 -> x0, other arithmetic: 37 us -> none  [the longest x1 28.4 us: body(): best = lax.top_k(scores, TOPK)[0]]
    concatenate x3 -> x2, other arithmetic: 19.7 us -> 48.2 us  [the longest x1 27.4 us: body(): jnp.roll(slab, -offset, axis=2)]
    reshape x1, local copies, waits for them, and re-layouts: 0.01 us -> 20.5 us  [body(): slab = templates.reshape(count, RAD, ANG)]
    reduce_sum x1 -> x0, other arithmetic: 10 us -> none  [body(): squares = jnp.sum(wide * wide, axis=1)]
    mul x3 -> x1, other arithmetic: 9.73 us -> 0.01 us  [body(): jnp.sum(jnp.where(owned[:, :, None], raw, 0.0), axis=3) * scale[:, :, None]]
    dot_general x0 -> x1, other arithmetic: none -> 7.41 us  [body(): jnp.einsum('mfp,mfp->mp', gathered, gathered, preferred_element_type=jnp....]
  transfers between devices with their start and end apart: 3 -> 3, of which waited for: 3 -> 2; matrix products, arithmetic and copies ran while one was open for 0% -> 33% of each run, Pallas kernels for 0% -> 0%
where the time goes in v2:
time: 404 us; the launch traced here: 402 us
  waiting for transfers between devices  145 us (36%)
  local copies, waits for them, and re-layouts  87.7 us (22%)
  other arithmetic  68.3 us (17%)
  blocking collectives  50.3 us (12%)
  matrix products  21.3 us (5%)
  between operations  14.1 us (3%)
  Pallas kernels  10.9 us (3%)
  starting transfers between devices  4.23 us (1%)
    reduce_scatter x1, waiting for transfers between devices, body(): lax.psum_scatter(bins.astype(jnp.bfloat16), 'orient', scatter_dimension=0...  141 us
    all_gather x1, blocking collectives, body(): everyone = lax.all_gather(merged, 'orient', axis=0)  50.3 us
    concatenate x2, local copies, waits for them, and re-layouts, body(): jnp.concatenate(turned, axis=0)  39.8 us
    concatenate x1, other arithmetic, body(): jnp.roll(slab, -offset, axis=2)  27.4 us
    slice x2, local copies, waits for them, and re-layouts, body(): jnp.roll(slab, -offset, axis=2)  24.1 us
    dot_general x1, matrix products, body(): lax.dot_general(gathered, rotated, (((1,), (1,)), ((), ())), preferred_el...  21.3 us
    concatenate x1, other arithmetic, body(): jnp.concatenate(turned, axis=0)  20.9 us
    reshape x1, local copies, waits for them, and re-layouts, body(): slab = templates.reshape(count, RAD, ANG)  20.5 us
  transfers between devices with their start and end apart: 3, of which 2 were waited for; matrix products, arithmetic and copies ran while one was open for 33% of the time, Pallas kernels for 0%

profile of v2, /device:TPU:1, one launch (start us, length us, event | category | flops | bytes accessed | tf_op | source)
XLA Modules:
  0.0 402.0 jit_solution(328314605036512929)
XLA Ops:
  7.2 10.9 %shard_map.77 = f32[12288,128]{1,0:T(8,128)} custom-call(bf16[128,1024]{1,0:T(8,128)(2,1)} %bitcast.185, f32[1,1024]{1,0:T(1,128)} %bitcast.186, f32[1,1024]{1,0:T(1,128)} %bitcast.187, s32[1,1024]{1,0:T(1,128)} %bitcast.188), custom_call_target="tpu_custom_call" | custom-call | flops 3221225472 | bytes 6553600 | tf_op jit(solution)/shard_map/pallas_call | solution.py:41
  18.1 4.2 %convert_element_type.3 = bf16[12288,128]{1,0:T(8,128)(2,1)} convert(f32[12288,128]{1,0:T(8,128)} %shard_map.77) | non-fusion elementwise | flops 1572864 | bytes 9437184 | tf_op jit(solution)/shard_map/convert_element_type | solution.py:91
  22.4 140.8 %reduce-scatter.2.cloned.1.call-done = bf16[192,128]{1,0:T(8,128)(2,1)} async-done(((bf16[12288,128]{1,0:T(8,128)(2,1)}), bf16[192,128]{1,0:T(8,128)(2,1)}) %reduce-scatter.2.cloned.1.call-update) | async-done | bytes 49168 | tf_op jit(solution)/shard_map/reduce_scatter | solution.py:91
  163.2 20.5 %reshape.892 = bf16[400,64,192]{2,1,0:T(8,128)(2,1)} reshape(bf16[400,12288]{1,0:T(8,128)(2,1)} %param.10) | data formatting | bytes 19660800 | tf_op jit(solution)/shard_map/reshape | solution.py:101
  183.7 12.3 %fusion.27 = (bf16[400,64,1]{2,1,0:T(8,128)(2,1)}, bf16[400,64,1]{2,1,0:T(8,128)(2,1)}) fusion(bf16[400,64,192]{2,1,0:T(8,128)(2,1)} %reshape.892), kind=kLoop, calls=%fused_computation.90 | loop fusion | bytes 204800 | tf_op jit(solution)/shard_map/jit(_roll_static)/slice | solution.py:102
  196.0 0.5 copy-done
  196.5 11.8 %fusion.28 = (bf16[400,64,191]{2,1,0:T(8,128)(2,1)}, bf16[400,64,191]{2,1,0:T(8,128)(2,1)}) fusion(bf16[400,64,192]{2,1,0:T(8,128)(2,1)S(1)} %copy-done), kind=kLoop, calls=%fused_computation.91 | loop fusion | bytes 39116800 | tf_op jit(solution)/shard_map/jit(_roll_static)/slice | solution.py:102
  208.3 27.4 %pad_maximum_fusion.1 = (bf16[400,64,192]{2,1,0:T(8,128)(2,1)}, bf16[400,64,192]{2,1,0:T(8,128)(2,1)}) fusion(bf16[400,64,191]{2,1,0:T(8,128)(2,1)} %get-tuple-element.4, bf16[400,64,1]{2,1,0:T(8,128)(2,1)} %get-tuple-element.2, bf16[400,64,1]{2,1,0:T(8,128)(2,1)} %get-tuple-element.3, bf16[400,64,191]{2,1,0:T(8,128)(2,1)} %get-tuple-element.5), kind=kLoop, calls=%fused_computation.3 | loop fusion | flops 39321600 | bytes 39321600 | tf_op jit(solution)/shard_map/jit(_roll_static)/concatenate | solution.py:102
  235.7 19.8 %concatenate.26 = bf16[400,12288]{1,0:T(8,128)(2,1)} reshape(bf16[400,64,192]{2,1,0:T(8,128)(2,1)} %get-tuple-element.8) | data formatting | bytes 19660800 | tf_op jit(solution)/shard_map/concatenate | solution.py:103
  255.5 20.1 %concatenate.28 = bf16[400,12288]{1,0:T(8,128)(2,1)} reshape(bf16[400,64,192]{2,1,0:T(8,128)(2,1)} %get-tuple-element.9) | data formatting | bytes 19660800 | tf_op jit(solution)/shard_map/concatenate | solution.py:103
  275.5 0.1 iota_compare_fusion
  275.7 20.9 %pad_maximum_fusion = bf16[1200,12288]{1,0:T(8,128)(2,1)} fusion(bf16[400,12288]{1,0:T(8,128)(2,1)} %concatenate.28, bf16[400,12288]{1,0:T(8,128)(2,1)} %param.10, bf16[400,12288]{1,0:T(8,128)(2,1)} %concatenate.26), kind=kLoop, calls=%fused_computation | loop fusion | flops 88473600 | bytes 58982400 | tf_op jit(solution)/shard_map/concatenate | solution.py:103
  296.6 7.4 %fusion = f32[4,128]{1,0:T(4,128)S(1)} fusion(bf16[4,128,12288]{1,2,0:T(8,128)(2,1)} %bitcast.155), kind=kLoop, calls=%fused_computation.2 | loop fusion | flops 18873856 | bytes 12584960 | tf_op jit(solution)/shard_map/mfp,mfp->mp/dot_general | solution.py:96
  304.0 21.3 %select_reduce_fusion = (f32[4,128,3]{1,2,0:T(4,128)S(1)}, f32[4,128,3,400]{1,3,2,0:T(8,128)S(1)}) fusion(pred[4,128,400]{1,2,0:T(8,128)(4,1)S(1)} %iota_compare_fusion, bf16[4,12288,128,1]{2,1,3,0:T(8,128)(2,1)} %bitcast.156, bf16[3,400,12288,1]{2,1,0,3:T(8,128)(2,1)} %bitcast.154), kind=kOutput, calls=%fused_computation.5 | convolution fusion | flops 15100721152 | bytes 44742656 | tf_op jit(solution)/shard_map/dot_general | solution.py:104
  325.4 0.2 select_reduce_fusion.8
  325.6 0.1 fusion.17
  325.7 0.2 select_reduce_fusion.7
  325.9 0.2 fusion.10
  326.1 0.3 select_reduce_fusion.6
  326.4 0.2 fusion.26
  326.6 0.3 select_reduce_fusion.5
  326.9 0.3 fusion.9
  327.2 0.4 select_reduce_fusion.4
  327.6 0.3 fusion.16
  327.9 0.4 select_reduce_fusion.3
  328.4 0.4 fusion.8
  328.8 0.5 select_reduce_fusion.2
  329.2 0.5 select_reduce_fusion.1
  329.7 1.2 concatenate.30
  330.9 4.1 %all-to-all-start = ((f32[4,128,11]{1,2,0:T(8,128)}), f32[4,128,11]{1,2,0:T(8,128)S(1)}, u32[]{:S(2)}, u32[]{:S(2)}) async-start(f32[4,128,11]{1,2,0:T(8,128)} %concatenate.30), calls=%async_computation.1 | async-start | bytes 65536 | tf_op jit(solution)/shard_map/all_to_all | solution.py:116
  335.1 4.3 %all-to-all-done = f32[4,128,11]{1,2,0:T(8,128)S(1)} async-done(((f32[4,128,11]{1,2,0:T(8,128)}), f32[4,128,11]{1,2,0:T(8,128)S(1)}, u32[]{:S(2)}, u32[]{:S(2)}) %all-to-all-start) | async-done | bytes 22560 | tf_op jit(solution)/shard_map/all_to_all | solution.py:116
  340.8 50.3 %all-gather = f32[8192,11]{0,1:T(8,128)S(1)} all-gather(f32[128,11]{0,1:T(8,128)S(1)} %concatenate.31), channel_id=2, replica_groups=mesh['section'=4,'orient'=64] {'orient'}, dimensions={0}, use_global_device_ids=true | all-gather | bytes 366080 | tf_op jit(solution)/shard_map/all_gather | solution.py:118
  391.3 0.1 select_reduce_fusion.16
  391.5 0.2 fusion.15
  391.6 0.2 select_reduce_fusion.15
  391.8 0.2 fusion.12
  392.0 0.2 select_reduce_fusion.14
  392.1 0.2 fusion.25
  392.3 0.2 select_reduce_fusion.13
  392.4 0.2 fusion.13
  392.6 0.2 select_reduce_fusion.12
  392.8 0.2 fusion.21
  393.0 0.2 select_reduce_fusion.11
  393.2 0.2 fusion.14
  393.4 0.2 select_reduce_fusion.10
  393.6 0.2 select_reduce_fusion.9
  393.9 0.7 copy.45
  394.5 0.6 concatenate.32
  (36 shorter events, 1.9 us)
Async XLA Ops:
  7.2 156.0 %reduce-scatter.2.cloned.1.call-start = ((), (), s32[]{:S(2)}) async-start(), calls=%async_computation.2 | async-start | bytes 3194880 | tf_op jit(solution)/shard_map/reduce_scatter | solution.py:91
  22.4 274.2 %all-gather.3.cloned.1.call-start = ((), (), s32[]{:S(2)}) async-start(), calls=%async_computation.3 | async-start | bytes 12632064 | tf_op jit(solution)/shard_map/all_gather | solution.py:92
  183.7 12.8 %copy-start = (bf16[400,64,192]{2,1,0:T(8,128)(2,1)S(1)}, bf16[400,64,192]{2,1,0:T(8,128)(2,1)}, u32[]{:S(2)}) copy-start(bf16[400,64,192]{2,1,0:T(8,128)(2,1)} %reshape.892) | copy-start | bytes 29491204
  255.5 20.1 %copy-start.1 = (s32[4,128]{1,0:T(4,128)S(1)}, s32[4,128]{1,0:T(4,128)}, u32[]{:S(2)}) copy-start(s32[4,128]{1,0:T(4,128)} %param.11) | copy-start | bytes 6148
  330.9 8.4 %all-to-all-start = ((f32[4,128,11]{1,2,0:T(8,128)}), f32[4,128,11]{1,2,0:T(8,128)S(1)}, u32[]{:S(2)}, u32[]{:S(2)}) async-start(f32[4,128,11]{1,2,0:T(8,128)} %concatenate.30), calls=%async_computation.1 | async-start | bytes 65536 | tf_op jit(solution)/shard_map/all_to_all | solution.py:116
Sparse Core Ops, SparseCore 0:
  22.5 140.6 reduce-scatter.1
  167.0 124.8 all-gather.2

commit v3 on v2

--- a/solution.py
+++ b/solution.py
@@ -88,7 +88,10 @@
     count = templates.shape[0]
 
     bins = bin_pixels(patterns[0], background, detector_gain, bin_map, features_total)
-    part = lax.psum_scatter(bins.astype(jnp.bfloat16), "orient", scatter_dimension=0, tiled=True)
+    pieces = lax.all_to_all(bins.astype(jnp.bfloat16), "orient", 0, 0, tiled=True)
+    part = jnp.sum(
+        pieces.reshape(orients, features_total // orients, patterns_per).astype(jnp.float32), axis=0
+    ).astype(jnp.bfloat16)
     gathered = lax.all_gather(
         part, ("section", "orient"), axis=0, tiled=True
     ).reshape(batches, features_total, patterns_per)

time: 404 us -> 345 us (0.85)
  waiting for transfers between devices: 145 us -> 4.33 us
  blocking collectives: 50.3 us -> 133 us
    reduce_scatter x1 -> x0, waiting for transfers between devices: 141 us -> none  [body(): lax.psum_scatter(bins.astype(jnp.bfloat16), 'orient', scatter_dimension=0...]
    all_to_all x0 -> x1, blocking collectives: none -> 85.6 us  [body(): lax.all_to_all(bins.astype(jnp.bfloat16), 'orient', 0, 0, tiled=True)]
  transfers between devices with their start and end apart: 3 -> 2, of which waited for: 2 -> 1; matrix products, arithmetic and copies ran while one was open for 33% -> 39% of each run, Pallas kernels for 0% -> 0%
where the time goes in v3:
time: 345 us; the launch traced here: 343 us
  blocking collectives  133 us (39%)
  local copies, waits for them, and re-layouts  87.8 us (25%)
  other arithmetic  68 us (20%)
  matrix products  21.3 us (6%)
  between operations  14.1 us (4%)
  Pallas kernels  10.9 us (3%)
  waiting for transfers between devices  4.33 us (1%)
  starting transfers between devices  4.06 us (1%)
    all_to_all x1, blocking collectives, body(): lax.all_to_all(bins.astype(jnp.bfloat16), 'orient', 0, 0, tiled=True)  85.6 us
    all_gather x1, blocking collectives, body(): everyone = lax.all_gather(merged, 'orient', axis=0)  47.3 us
    concatenate x2, local copies, waits for them, and re-layouts, body(): jnp.concatenate(turned, axis=0)  39.9 us
    concatenate x1, other arithmetic, body(): jnp.roll(slab, -offset, axis=2)  27.4 us
    slice x2, local copies, waits for them, and re-layouts, body(): jnp.roll(slab, -offset, axis=2)  24.1 us
    dot_general x1, matrix products, body(): lax.dot_general(gathered, rotated, (((1,), (1,)), ((), ())), preferred_el...  21.3 us
    concatenate x1, other arithmetic, body(): jnp.concatenate(turned, axis=0)  20.8 us
    reshape x1, local copies, waits for them, and re-layouts, body(): slab = templates.reshape(count, RAD, ANG)  20.5 us
  transfers between devices with their start and end apart: 2, of which 1 were waited for; matrix products, arithmetic and copies ran while one was open for 39% of the time, Pallas kernels for 0%

profile of v3, /device:TPU:1, one launch (start us, length us, event | category | flops | bytes accessed | tf_op | source)
XLA Modules:
  0.0 343.4 jit_solution(3487181158186032309)
XLA Ops:
  7.2 10.9 %shard_map.77 = f32[12288,128]{1,0:T(8,128)} custom-call(bf16[128,1024]{1,0:T(8,128)(2,1)} %bitcast.187, f32[1,1024]{1,0:T(1,128)} %bitcast.188, f32[1,1024]{1,0:T(1,128)} %bitcast.189, s32[1,1024]{1,0:T(1,128)} %bitcast.190), custom_call_target="tpu_custom_call" | custom-call | flops 3221225472 | bytes 6553600 | tf_op jit(solution)/shard_map/pallas_call | solution.py:41
  18.1 3.0 convert_element_type.2
  21.1 85.6 %all_to_all.14 = bf16[64,192,128]{2,1,0:T(8,128)(2,1)S(1)} all-to-all(bf16[64,192,128]{2,1,0:T(8,128)(2,1)S(1)} %bitcast.158), channel_id=1, replica_groups=mesh['section'=4,'orient'=64] {'orient'}, dimensions={0} | all-to-all | bytes 6291456 | tf_op jit(solution)/shard_map/all_to_all | solution.py:91
  106.7 1.1 reduce_sum.39
  107.8 20.5 %reshape.896 = bf16[400,64,192]{2,1,0:T(8,128)(2,1)} reshape(bf16[400,12288]{1,0:T(8,128)(2,1)} %param.10) | data formatting | bytes 19660800 | tf_op jit(solution)/shard_map/reshape | solution.py:104
  128.4 12.3 %fusion.27 = (bf16[400,64,1]{2,1,0:T(8,128)(2,1)}, bf16[400,64,1]{2,1,0:T(8,128)(2,1)}) fusion(bf16[400,64,192]{2,1,0:T(8,128)(2,1)} %reshape.896), kind=kLoop, calls=%fused_computation.90 | loop fusion | bytes 204800 | tf_op jit(solution)/shard_map/jit(_roll_static)/slice | solution.py:105
  140.6 0.5 copy-done
  141.2 11.8 %fusion.28 = (bf16[400,64,191]{2,1,0:T(8,128)(2,1)}, bf16[400,64,191]{2,1,0:T(8,128)(2,1)}) fusion(bf16[400,64,192]{2,1,0:T(8,128)(2,1)S(1)} %copy-done), kind=kLoop, calls=%fused_computation.91 | loop fusion | bytes 39116800 | tf_op jit(solution)/shard_map/jit(_roll_static)/slice | solution.py:105
  153.0 27.4 %pad_maximum_fusion.1 = (bf16[400,64,192]{2,1,0:T(8,128)(2,1)}, bf16[400,64,192]{2,1,0:T(8,128)(2,1)}) fusion(bf16[400,64,191]{2,1,0:T(8,128)(2,1)} %get-tuple-element.4, bf16[400,64,1]{2,1,0:T(8,128)(2,1)} %get-tuple-element.2, bf16[400,64,1]{2,1,0:T(8,128)(2,1)} %get-tuple-element.3, bf16[400,64,191]{2,1,0:T(8,128)(2,1)} %get-tuple-element.5), kind=kLoop, calls=%fused_computation.3 | loop fusion | flops 39321600 | bytes 39321600 | tf_op jit(solution)/shard_map/jit(_roll_static)/concatenate | solution.py:105
  180.3 19.8 %concatenate.26 = bf16[400,12288]{1,0:T(8,128)(2,1)} reshape(bf16[400,64,192]{2,1,0:T(8,128)(2,1)} %get-tuple-element.8) | data formatting | bytes 19660800 | tf_op jit(solution)/shard_map/concatenate | solution.py:106
  200.2 20.0 %concatenate.28 = bf16[400,12288]{1,0:T(8,128)(2,1)} reshape(bf16[400,64,192]{2,1,0:T(8,128)(2,1)} %get-tuple-element.9) | data formatting | bytes 19660800 | tf_op jit(solution)/shard_map/concatenate | solution.py:106
  220.3 20.8 %pad_maximum_fusion = bf16[1200,12288]{1,0:T(8,128)(2,1)} fusion(bf16[400,12288]{1,0:T(8,128)(2,1)} %concatenate.28, bf16[400,12288]{1,0:T(8,128)(2,1)} %param.10, bf16[400,12288]{1,0:T(8,128)(2,1)} %concatenate.26), kind=kLoop, calls=%fused_computation | loop fusion | flops 88473600 | bytes 58982400 | tf_op jit(solution)/shard_map/concatenate | solution.py:106
  241.1 7.4 %fusion = f32[4,128]{1,0:T(4,128)S(1)} fusion(bf16[4,128,12288]{1,2,0:T(8,128)(2,1)} %bitcast.156), kind=kLoop, calls=%fused_computation.2 | loop fusion | flops 18873856 | bytes 12584960 | tf_op jit(solution)/shard_map/mfp,mfp->mp/dot_general | solution.py:99
  248.6 21.3 %select_reduce_fusion = (f32[4,128,3]{1,2,0:T(4,128)S(1)}, f32[4,128,3,400]{1,3,2,0:T(8,128)S(1)}) fusion(pred[4,128,400]{1,2,0:T(8,128)(4,1)S(1)} %iota_compare_fusion, bf16[4,12288,128,1]{2,1,3,0:T(8,128)(2,1)} %bitcast.157, bf16[3,400,12288,1]{2,1,0,3:T(8,128)(2,1)} %bitcast.155), kind=kOutput, calls=%fused_computation.5 | convolution fusion | flops 15100721152 | bytes 44742656 | tf_op jit(solution)/shard_map/dot_general | solution.py:107
  270.0 0.2 select_reduce_fusion.8
  270.1 0.1 fusion.17
  270.3 0.2 select_reduce_fusion.7
  270.5 0.2 fusion.10
  270.7 0.3 select_reduce_fusion.6
  270.9 0.2 fusion.26
  271.2 0.3 select_reduce_fusion.5
  271.5 0.3 fusion.9
  271.8 0.4 select_reduce_fusion.4
  272.2 0.3 fusion.16
  272.5 0.4 select_reduce_fusion.3
  272.9 0.4 fusion.8
  273.3 0.5 select_reduce_fusion.2
  273.8 0.5 select_reduce_fusion.1
  274.3 1.2 concatenate.30
  275.5 4.0 %all-to-all-start.1 = ((f32[4,128,11]{1,2,0:T(8,128)}), f32[4,128,11]{1,2,0:T(8,128)S(1)}, u32[]{:S(2)}, u32[]{:S(2)}) async-start(f32[4,128,11]{1,2,0:T(8,128)} %concatenate.30), calls=%async_computation.1 | async-start | bytes 65536 | tf_op jit(solution)/shard_map/all_to_all | solution.py:119
  279.6 4.3 %all-to-all-done.1 = f32[4,128,11]{1,2,0:T(8,128)S(1)} async-done(((f32[4,128,11]{1,2,0:T(8,128)}), f32[4,128,11]{1,2,0:T(8,128)S(1)}, u32[]{:S(2)}, u32[]{:S(2)}) %all-to-all-start.1) | async-done | bytes 22560 | tf_op jit(solution)/shard_map/all_to_all | solution.py:119
  285.2 47.3 %all-gather = f32[8192,11]{0,1:T(8,128)S(1)} all-gather(f32[128,11]{0,1:T(8,128)S(1)} %concatenate.31), channel_id=2, replica_groups=mesh['section'=4,'orient'=64] {'orient'}, dimensions={0}, use_global_device_ids=true | all-gather | bytes 366080 | tf_op jit(solution)/shard_map/all_gather | solution.py:121
  332.8 0.1 select_reduce_fusion.16
  332.9 0.2 fusion.15
  333.1 0.2 select_reduce_fusion.15
  333.2 0.2 fusion.12
  333.4 0.2 select_reduce_fusion.14
  333.5 0.2 fusion.25
  333.7 0.2 select_reduce_fusion.13
  333.9 0.2 fusion.13
  334.0 0.2 select_reduce_fusion.12
  334.2 0.2 fusion.21
  334.4 0.2 select_reduce_fusion.11
  334.6 0.2 fusion.14
  334.8 0.2 select_reduce_fusion.10
  335.0 0.2 select_reduce_fusion.9
  335.3 0.7 copy.45
  336.0 0.6 concatenate.32
  (35 shorter events, 2.0 us)
Async XLA Ops:
  7.2 234.0 %all-gather.3.cloned.1.call-start = ((), (), s32[]{:S(2)}) async-start(), calls=%async_computation.2 | async-start | bytes 12632064 | tf_op jit(solution)/shard_map/all_gather | solution.py:95
  128.4 12.8 %copy-start = (bf16[400,64,192]{2,1,0:T(8,128)(2,1)S(1)}, bf16[400,64,192]{2,1,0:T(8,128)(2,1)}, u32[]{:S(2)}) copy-start(bf16[400,64,192]{2,1,0:T(8,128)(2,1)} %reshape.896) | copy-start | bytes 29491204
  200.2 20.1 %copy-start.1 = (s32[4,128]{1,0:T(4,128)S(1)}, s32[4,128]{1,0:T(4,128)}, u32[]{:S(2)}) copy-start(s32[4,128]{1,0:T(4,128)} %param.11) | copy-start | bytes 6148
  275.5 8.3 %all-to-all-start.1 = ((f32[4,128,11]{1,2,0:T(8,128)}), f32[4,128,11]{1,2,0:T(8,128)S(1)}, u32[]{:S(2)}, u32[]{:S(2)}) async-start(f32[4,128,11]{1,2,0:T(8,128)} %concatenate.30), calls=%async_computation.1 | async-start | bytes 65536 | tf_op jit(solution)/shard_map/all_to_all | solution.py:119
Sparse Core Ops, SparseCore 0:
  107.9 118.5 all-gather.2

commit v4 on v3

--- a/solution.py
+++ b/solution.py
@@ -101,19 +101,23 @@
     )
     scale = lax.rsqrt(squares / features_total + EPS)
 
-    slab = templates.reshape(count, RAD, ANG)
-    turned = [jnp.roll(slab, -offset, axis=2) for offset in range(-REACH, REACH + 1)]
-    rotated = jnp.concatenate(turned, axis=0).reshape((2 * REACH + 1) * count, features_total)
-    raw = lax.dot_general(
-        gathered, rotated, (((1,), (1,)), ((), ())), preferred_element_type=jnp.float32
-    ).reshape(batches, patterns_per, 2 * REACH + 1, count)
-    scores = raw[:, :, REACH] * scale[:, :, None]
-    best = top_values(scores)
-
     group_base = (section_index * orients + orient_index) * count
     local = best_picks - group_base
     owned = local[:, :, None] == lax.broadcasted_iota(jnp.int32, (batches, patterns_per, count), 2)
-    picked = jnp.sum(jnp.where(owned[:, :, None], raw, 0.0), axis=3) * scale[:, :, None]
+    chosen = jnp.einsum(
+        "tf,mpt->mfp", templates, owned.astype(jnp.bfloat16), preferred_element_type=jnp.float32
+    ).reshape(batches, RAD, ANG, patterns_per)
+    rings = gathered.reshape(batches, RAD, ANG, patterns_per).astype(jnp.float32)
+    columns = [
+        jnp.sum(rings * jnp.roll(chosen, -offset, axis=2), axis=(1, 2))
+        for offset in range(-REACH, REACH + 1)
+    ]
+    picked = jnp.stack(columns, axis=-1) * scale[:, :, None]
+
+    raw = lax.dot_general(
+        gathered, templates, (((1,), (1,)), ((), ())), preferred_element_type=jnp.float32
+    )
+    best = top_values(raw * scale[:, :, None])
     packed = jnp.concatenate([best, picked], axis=-1)
 
     mine = lax.all_to_all(packed, "section", 0, 0, tiled=True)

time: 345 us -> 384 us (1.11)
  waiting for transfers between devices: 4.33 us -> 123 us
  local copies, waits for them, and re-layouts: 87.8 us -> 40.3 us
  other arithmetic: 68 us -> 36.6 us
    all_gather x1, waiting for transfers between devices: 0.02 us -> 119 us  [body(): lax.all_gather(part, ('section', 'orient'), axis=0, tiled=True)]
    concatenate x2 -> x0, other arithmetic: 48.1 us -> none  [the longest x1 27.4 us: body(): jnp.roll(slab, -offset, axis=2)]
    concatenate x2 -> x0, local copies, waits for them, and re-layouts: 39.9 us -> none  [body(): jnp.concatenate(turned, axis=0)]
    reduce_sum x0 -> x1, other arithmetic: none -> 21.3 us  [body(): jnp.sum(rings * jnp.roll(chosen, -offset, axis=2), axis=(1, 2))]
    reshape x1 -> x0, local copies, waits for them, and re-layouts: 20.5 us -> none  [body(): slab = templates.reshape(count, RAD, ANG)]
    slice x2, local copies, waits for them, and re-layouts: 24.1 us -> 37.5 us  [body(): jnp.roll(chosen, -offset, axis=2)]
    dot_general x1, other arithmetic: 7.41 us -> 3.4 us  [body(): jnp.einsum('mfp,mfp->mp', gathered, gathered, preferred_element_type=jnp....]
    dot_general x1 -> x2, matrix products: 21.3 us -> 24.7 us  [the longest x1 16.2 us: body(): jnp.einsum('tf,mpt->mfp', templates, owned.astype(jnp.bfloat16), preferre...]
  transfers between devices with their start and end apart: 2 -> 2, of which waited for: 1 -> 2; matrix products, arithmetic and copies ran while one was open for 39% -> 0% of each run, Pallas kernels for 0% -> 0%
where the time goes in v4:
time: 384 us
  blocking collectives  130 us (34%)
  waiting for transfers between devices  123 us (32%)
  local copies, waits for them, and re-layouts  40.3 us (10%)
  other arithmetic  36.6 us (10%)
  matrix products  24.7 us (6%)
  between operations  14.2 us (4%)
  Pallas kernels  10.9 us (3%)
  starting transfers between devices  4.02 us (1%)
    all_gather x1, waiting for transfers between devices, body(): lax.all_gather(part, ('section', 'orient'), axis=0, tiled=True)  119 us
    all_to_all x1, blocking collectives, body(): lax.all_to_all(bins.astype(jnp.bfloat16), 'orient', 0, 0, tiled=True)  85.6 us
    all_gather x1, blocking collectives, body(): everyone = lax.all_gather(merged, 'orient', axis=0)  44.8 us
    slice x2, local copies, waits for them, and re-layouts, body(): jnp.roll(chosen, -offset, axis=2)  37.5 us
    reduce_sum x1, other arithmetic, body(): jnp.sum(rings * jnp.roll(chosen, -offset, axis=2), axis=(1, 2))  21.3 us
    dot_general x1, matrix products, body(): jnp.einsum('tf,mpt->mfp', templates, owned.astype(jnp.bfloat16), preferre...  16.2 us
    pallas_call x1, Pallas kernels, bin_pixels(): pl.pallas_call(bin_kernel, grid=(total // height,), in_specs=[pl.BlockSpe...  10.9 us
    dot_general x1, matrix products, body(): lax.dot_general(gathered, templates, (((1,), (1,)), ((), ())), preferred_...  8.48 us
  transfers between devices with their start and end apart: 2, of which 2 were waited for; matrix products, arithmetic and copies ran while one was open for 0% of the time, Pallas kernels for 0%

profile of v4, /device:TPU:1, one launch (start us, length us, event | category | flops | bytes accessed | tf_op | source)
XLA Modules:
  0.0 384.0 jit_solution(4500176190868131367)
XLA Ops:
  7.2 10.9 %shard_map.77 = f32[12288,128]{1,0:T(8,128)} custom-call(bf16[128,1024]{1,0:T(8,128)(2,1)} %bitcast.169, f32[1,1024]{1,0:T(1,128)} %bitcast.170, f32[1,1024]{1,0:T(1,128)} %bitcast.171, s32[1,1024]{1,0:T(1,128)} %bitcast.172), custom_call_target="tpu_custom_call" | custom-call | flops 3221225472 | bytes 6553600 | tf_op jit(solution)/shard_map/pallas_call | solution.py:41
  18.1 3.0 convert_element_type.15
  21.1 85.6 %all_to_all.14 = bf16[64,192,128]{2,1,0:T(8,128)(2,1)S(1)} all-to-all(bf16[64,192,128]{2,1,0:T(8,128)(2,1)S(1)} %bitcast.137), channel_id=1, replica_groups=mesh['section'=4,'orient'=64] {'orient'}, dimensions={0} | all-to-all | bytes 6291456 | tf_op jit(solution)/shard_map/all_to_all | solution.py:91
  106.7 1.1 reduce_sum.57
  107.9 118.7 %all-gather.3.cloned.1.call-done = bf16[49152,128]{1,0:T(8,128)(2,1)} async-done(((bf16[192,128]{1,0:T(8,128)(2,1)}), bf16[49152,128]{1,0:T(8,128)(2,1)}) %all-gather.3.cloned.1.call-update) | async-done | bytes 12582928 | tf_op jit(solution)/shard_map/all_gather | solution.py:95
  226.6 16.2 %fusion.2 = (f32[4,128]{1,0:T(4,128)S(1)}, f32[4,128,12288]{1,2,0:T(8,128)}) fusion(bf16[4,12288,128]{2,1,0:T(8,128)(2,1)} %bitcast.133, bf16[400,12288]{1,0:T(8,128)(2,1)} %param.10, s32[4,128]{1,0:T(4,128)S(1)} %broadcast_subtract_fusion), kind=kOutput, calls=%fused_computation.5 | convolution fusion | flops 5052243456 | bytes 47583232 | tf_op jit(solution)/shard_map/tf,mpt->mfp/dot_general | solution.py:107
  242.8 35.6 %fusion.36 = (f32[4,64,191,128]{3,2,1,0:T(8,128)}, f32[4,64,191,128]{3,2,1,0:T(8,128)}) fusion(f32[4,64,192,128]{3,2,1,0:T(8,128)} %bitcast.131), kind=kLoop, calls=%fused_computation.95 | loop fusion | bytes 100139008 | tf_op jit(solution)/shard_map/jit(_roll_static)/slice | solution.py:112
  278.3 1.9 fusion.37
  280.3 3.4 fusion.3
  283.7 8.5 %fusion.38 = (f32[4,128]{1,0:T(4,128)S(1)}, f32[4,128,400]{1,2,0:T(8,128)S(1)}) fusion(f32[4,128]{1,0:T(4,128)S(1)} %add_rsqrt_fusion, bf16[4,12288,128]{2,1,0:T(8,128)(2,1)S(1)} %bitcast.135, bf16[400,12288]{1,0:T(8,128)(2,1)} %param.10), kind=kOutput, calls=%fused_computation.97 | convolution fusion | flops 5033573888 | bytes 23236608 | tf_op jit(solution)/shard_map/dot_general | solution.py:117
  292.2 0.1 select_reduce_fusion.7
  292.3 0.1 fusion.20
  292.4 0.2 select_reduce_fusion.6
  292.6 0.2 fusion.19
  292.8 0.2 select_reduce_fusion.5
  293.0 0.2 fusion.35
  293.2 0.3 select_reduce_fusion.4
  293.5 0.3 fusion.18
  293.8 0.3 select_reduce_fusion.3
  294.1 0.3 fusion.26
  294.4 0.4 select_reduce_fusion.2
  294.8 0.4 fusion.17
  295.2 0.4 select_reduce_fusion.1
  295.7 0.4 select_reduce_fusion
  296.1 21.3 %fusion = (f32[4,128]{1,0:T(4,128)S(1)}, f32[4,128]{1,0:T(4,128)S(1)}) fusion(bf16[4,64,192,128]{3,2,1,0:T(8,128)(2,1)S(1)} %bitcast.136, f32[4,64,191,128]{3,2,1,0:T(8,128)} %get-tuple-element.5, f32[4,64,1,128]{3,2,1,0:T(1,128)S(1)} %get-tuple-element.7, f32[4,64,1,128]{3,2,1,0:T(1,128)S(1)} %get-tuple-element.6, f32[4,64,191,128]{3,2,1,0:T(8,128)} %get-tuple-element.4), kind=kLoop, calls=%fused_computation.2 | loop fusion | flops 44039168 | bytes 62918656 | tf_op jit(solution)/shard_map/reduce_sum | solution.py:112
  317.4 1.2 concatenate.19
  318.7 4.0 %all-to-all-start.1 = ((f32[4,128,11]{1,2,0:T(8,128)}), f32[4,128,11]{1,2,0:T(8,128)S(1)}, u32[]{:S(2)}, u32[]{:S(2)}) async-start(f32[4,128,11]{1,2,0:T(8,128)} %concatenate.19), calls=%async_computation.1 | async-start | bytes 65536 | tf_op jit(solution)/shard_map/all_to_all | solution.py:123
  322.7 4.3 %all-to-all-done.1 = f32[4,128,11]{1,2,0:T(8,128)S(1)} async-done(((f32[4,128,11]{1,2,0:T(8,128)}), f32[4,128,11]{1,2,0:T(8,128)S(1)}, u32[]{:S(2)}, u32[]{:S(2)}) %all-to-all-start.1) | async-done | bytes 22560 | tf_op jit(solution)/shard_map/all_to_all | solution.py:123
  328.0 0.1 fusion.29
  328.2 0.1 select_reduce_fusion.16
  328.4 44.8 %all-gather = f32[8192,11]{0,1:T(8,128)S(1)} all-gather(f32[128,11]{0,1:T(8,128)S(1)} %concatenate.20), channel_id=2, replica_groups=mesh['section'=4,'orient'=64] {'orient'}, dimensions={0}, use_global_device_ids=true | all-gather | bytes 366080 | tf_op jit(solution)/shard_map/all_gather | solution.py:125
  373.1 0.1 copy.27
  373.4 0.1 select_reduce_fusion.15
  373.5 0.2 fusion.25
  373.7 0.2 select_reduce_fusion.14
  373.8 0.2 fusion.22
  374.0 0.2 select_reduce_fusion.13
  374.1 0.2 fusion.34
  374.3 0.2 select_reduce_fusion.12
  374.5 0.2 fusion.23
  374.6 0.2 select_reduce_fusion.11
  374.8 0.2 fusion.30
  375.0 0.2 select_reduce_fusion.10
  375.2 0.2 fusion.24
  375.4 0.2 select_reduce_fusion.9
  375.6 0.2 select_reduce_fusion.8
  375.9 0.7 copy.19
  376.6 0.6 concatenate.21
  (30 shorter events, 1.5 us)
Async XLA Ops:
  7.2 100.7 %copy-start.1 = (s32[4,128]{1,0:T(4,128)S(1)}, s32[4,128]{1,0:T(4,128)}, u32[]{:S(2)}) copy-start(s32[4,128]{1,0:T(4,128)} %param.11) | copy-start | bytes 6148
  7.2 219.4 %all-gather.3.cloned.1.call-start = ((), (), s32[]{:S(2)}) async-start(), calls=%async_computation.2 | async-start | bytes 12632064 | tf_op jit(solution)/shard_map/all_gather | solution.py:95
  242.8 37.5 %copy-start = (bf16[49152,128]{1,0:T(8,128)(2,1)S(1)}, bf16[49152,128]{1,0:T(8,128)(2,1)}, u32[]{:S(2)}) copy-start(bf16[49152,128]{1,0:T(8,128)(2,1)} %all-gather.3.cloned.1.call-done) | copy-start | bytes 37748740
  318.7 8.3 %all-to-all-start.1 = ((f32[4,128,11]{1,2,0:T(8,128)}), f32[4,128,11]{1,2,0:T(8,128)S(1)}, u32[]{:S(2)}, u32[]{:S(2)}) async-start(f32[4,128,11]{1,2,0:T(8,128)} %concatenate.19), calls=%async_computation.1 | async-start | bytes 65536 | tf_op jit(solution)/shard_map/all_to_all | solution.py:123
Sparse Core Ops, SparseCore 0:
  108.0 118.5 all-gather.2

commit v5 on v4

--- a/solution.py
+++ b/solution.py
@@ -70,6 +70,20 @@
     return jnp.concatenate(found, axis=-1)
 
 
+def rotated_dot(rings, chosen, offset):
+    width = rings.shape[2]
+    spans = [(0, width)] if offset == 0 else (
+        [(0, width - offset), (width - offset, width)] if offset > 0 else [(0, -offset), (-offset, width)]
+    )
+    total = 0.0
+    for low, high in spans:
+        near = lax.slice_in_dim(rings, low, high, axis=2).astype(jnp.float32)
+        far_low = (low + offset) % width
+        far = lax.slice_in_dim(chosen, far_low, far_low + high - low, axis=2).astype(jnp.float32)
+        total = total + jnp.sum(near * far, axis=(1, 2))
+    return total
+
+
 def merge_packed(stack, axis):
     best = jnp.moveaxis(stack[..., :TOPK], axis, -2)
     best = best.reshape(best.shape[:-2] + (best.shape[-2] * TOPK,))
@@ -106,13 +120,12 @@
     owned = local[:, :, None] == lax.broadcasted_iota(jnp.int32, (batches, patterns_per, count), 2)
     chosen = jnp.einsum(
         "tf,mpt->mfp", templates, owned.astype(jnp.bfloat16), preferred_element_type=jnp.float32
-    ).reshape(batches, RAD, ANG, patterns_per)
-    rings = gathered.reshape(batches, RAD, ANG, patterns_per).astype(jnp.float32)
-    columns = [
-        jnp.sum(rings * jnp.roll(chosen, -offset, axis=2), axis=(1, 2))
-        for offset in range(-REACH, REACH + 1)
-    ]
-    picked = jnp.stack(columns, axis=-1) * scale[:, :, None]
+    ).astype(jnp.bfloat16)
+    chosen = lax.optimization_barrier(chosen).reshape(batches, RAD, ANG, patterns_per)
+    rings = gathered.reshape(batches, RAD, ANG, patterns_per)
+    picked = jnp.stack(
+        [rotated_dot(rings, chosen, offset) for offset in range(-REACH, REACH + 1)], axis=-1
+    ) * scale[:, :, None]
 
     raw = lax.dot_general(
         gathered, templates, (((1,), (1,)), ((), ())), preferred_element_type=jnp.float32
@@ -122,7 +135,9 @@
 
     mine = lax.all_to_all(packed, "section", 0, 0, tiled=True)
     merged = merge_packed(mine, 0)
-    everyone = lax.all_gather(merged, "orient", axis=0)
+    everyone = lax.all_to_all(
+        jnp.broadcast_to(merged[None], (orients,) + merged.shape), "orient", 0, 0
+    )
     final = merge_packed(everyone, 0)
     share = patterns_per // orients
     rows = lax.dynamic_slice_in_dim(final[:, TOPK:], orient_index * share, share, axis=0)

time: 384 us -> 321 us (0.84)
  blocking collectives: 130 us -> 85.6 us
  local copies, waits for them, and re-layouts: 40.3 us -> 20.9 us
  waiting for transfers between devices: 123 us -> 111 us
  starting transfers between devices: 4.02 us -> 12 us
  other arithmetic: 36.6 us -> 43.7 us
    all_gather x1 -> x0, blocking collectives: 44.8 us -> none  [body(): everyone = lax.all_gather(merged, 'orient', axis=0)]
    slice x2 -> x0, local copies, waits for them, and re-layouts: 37.5 us -> none  [body(): jnp.roll(chosen, -offset, axis=2)]
    all_gather x1, waiting for transfers between devices: 119 us -> 88.6 us  [body(): lax.all_gather(part, ('section', 'orient'), axis=0, tiled=True)]
    all_to_all x0 -> x1, waiting for transfers between devices: none -> 17.7 us  [body(): lax.all_to_all(jnp.broadcast_to(merged[None], (orients,) + merged.shape),...]
    optimization_barrier x0 -> x1, local copies, waits for them, and re-layouts: none -> 16.6 us  [body(): lax.optimization_barrier(chosen).reshape(batches, RAD, ANG, patterns_per)]
    all_to_all x0 -> x1, starting transfers between devices: none -> 8 us  [body(): lax.all_to_all(jnp.broadcast_to(merged[None], (orients,) + merged.shape),...]
    reduce_sum x1 -> x3, other arithmetic: 21.3 us -> 28.4 us  [rotated_dot(): total = total + jnp.sum(near * far, axis=(1, 2))]
  transfers between devices with their start and end apart: 2 -> 3, of which waited for: 2 -> 3; matrix products, arithmetic and copies ran while one was open for 0% -> 9% of each run, Pallas kernels for 0% -> 0%
where the time goes in v5:
time: 321 us; the launch traced here: 320 us
  waiting for transfers between devices  111 us (35%)
  blocking collectives  85.6 us (27%)
  other arithmetic  43.7 us (14%)
  matrix products  22 us (7%)
  local copies, waits for them, and re-layouts  20.9 us (7%)
  between operations  14.2 us (4%)
  starting transfers between devices  12 us (4%)
  Pallas kernels  10.9 us (3%)
    all_gather x1, waiting for transfers between devices, body(): lax.all_gather(part, ('section', 'orient'), axis=0, tiled=True)  88.6 us
    all_to_all x1, blocking collectives, body(): lax.all_to_all(bins.astype(jnp.bfloat16), 'orient', 0, 0, tiled=True)  85.6 us
    reduce_sum x3, other arithmetic, rotated_dot(): total = total + jnp.sum(near * far, axis=(1, 2))  28.4 us
    all_to_all x1, waiting for transfers between devices, body(): lax.all_to_all(jnp.broadcast_to(merged[None], (orients,) + merged.shape),...  17.7 us
    optimization_barrier x1, local copies, waits for them, and re-layouts, body(): lax.optimization_barrier(chosen).reshape(batches, RAD, ANG, patterns_per)  16.6 us
    dot_general x1, matrix products, body(): jnp.einsum('tf,mpt->mfp', templates, owned.astype(jnp.bfloat16), preferre...  13.5 us
    pallas_call x1, Pallas kernels, bin_pixels(): pl.pallas_call(bin_kernel, grid=(total // height,), in_specs=[pl.BlockSpe...  10.9 us
    dot_general x1, matrix products, body(): lax.dot_general(gathered, templates, (((1,), (1,)), ((), ())), preferred_...  8.48 us
  transfers between devices with their start and end apart: 3, of which 3 were waited for; matrix products, arithmetic and copies ran while one was open for 9% of the time, Pallas kernels for 0%

profile of v5, /device:TPU:1, one launch (start us, length us, event | category | flops | bytes accessed | tf_op | source)
XLA Modules:
  0.0 319.9 jit_solution(7281189209193116252)
XLA Ops:
  7.2 10.9 %shard_map.77 = f32[12288,128]{1,0:T(8,128)} custom-call(bf16[128,1024]{1,0:T(8,128)(2,1)} %bitcast.157, f32[1,1024]{1,0:T(1,128)} %bitcast.158, f32[1,1024]{1,0:T(1,128)} %bitcast.159, s32[1,1024]{1,0:T(1,128)} %bitcast.160), custom_call_target="tpu_custom_call" | custom-call | flops 3221225472 | bytes 6553600 | tf_op jit(solution)/shard_map/pallas_call | solution.py:41
  18.1 3.0 convert_element_type.42
  21.1 85.6 %all_to_all.19 = bf16[64,192,128]{2,1,0:T(8,128)(2,1)S(1)} all-to-all(bf16[64,192,128]{2,1,0:T(8,128)(2,1)S(1)} %bitcast.127), channel_id=1, replica_groups=mesh['section'=4,'orient'=64] {'orient'}, dimensions={0} | all-to-all | bytes 6291456 | tf_op jit(solution)/shard_map/all_to_all | solution.py:105
  106.7 1.1 reduce_sum.75
  107.9 13.5 %fusion.1 = bf16[4,12288,128]{1,2,0:T(8,128)(2,1)} fusion(bf16[400,12288]{1,0:T(8,128)(2,1)} %param.10, s32[4,128]{1,0:T(4,128)S(1)} %broadcast_subtract_fusion), kind=kOutput, calls=%fused_computation.6 | convolution fusion | flops 5039661056 | bytes 22415360 | tf_op jit(solution)/shard_map/tf,mpt->mfp/dot_general | solution.py:121
  121.4 16.6 %copy.31 = bf16[4,12288,128]{2,1,0:T(8,128)(2,1)} copy(bf16[4,12288,128]{1,2,0:T(8,128)(2,1)} %fusion.1) | data formatting | bytes 25165824 | tf_op jit(solution)/shard_map/optimization_barrier | solution.py:124
  138.0 88.6 %all-gather.2.cloned.1.call-done = bf16[49152,128]{1,0:T(8,128)(2,1)} async-done(((bf16[192,128]{1,0:T(8,128)(2,1)}), bf16[49152,128]{1,0:T(8,128)(2,1)}) %all-gather.2.cloned.1.call-update) | async-done | bytes 12582928 | tf_op jit(solution)/shard_map/all_gather | solution.py:109
  226.6 22.6 %multiply_reduce_fusion.2 = (f32[4,128]{1,0:T(4,128)S(1)}, f32[4,128]{1,0:T(4,128)S(1)}) fusion(bf16[4,64,192,128]{3,2,1,0:T(8,128)(2,1)} %bitcast.124, bf16[4,64,192,128]{3,2,1,0:T(8,128)(2,1)} %bitcast.119), kind=kLoop, calls=%fused_computation.4 | loop fusion | flops 50068480 | bytes 50073600 | tf_op jit(solution)/shard_map/reduce_sum | solution.py:83
  249.2 0.8 copy-done.1
  250.0 0.5 fusion.24
  250.5 5.3 %multiply_reduce_fusion.1 = f32[4,128]{1,0:T(4,128)S(1)} fusion(bf16[4,64,192,128]{3,2,1,0:T(8,128)(2,1)S(1)} %bitcast.126, bf16[4,64,192,128]{3,2,1,0:T(8,128)(2,1)S(1)} %bitcast.121), kind=kLoop, calls=%fused_computation.3 | loop fusion | flops 25165312 | bytes 25167872 | tf_op jit(solution)/shard_map/reduce_sum | solution.py:83
  255.8 3.4 %fusion = f32[4,128]{1,0:T(4,128)S(1)} fusion(bf16[4,128,12288]{1,2,0:T(8,128)(2,1)S(1)} %bitcast.122), kind=kLoop, calls=%fused_computation.1 | loop fusion | flops 18873856 | bytes 12584960 | tf_op jit(solution)/shard_map/mfp,mfp->mp/dot_general | solution.py:113
  259.2 8.5 %fusion.37 = (f32[4,128]{1,0:T(4,128)S(1)}, f32[4,128,400]{1,2,0:T(8,128)S(1)}) fusion(f32[4,128]{1,0:T(4,128)S(1)} %add_rsqrt_fusion, bf16[4,12288,128]{2,1,0:T(8,128)(2,1)S(1)} %bitcast.123, bf16[400,12288]{1,0:T(8,128)(2,1)} %param.10), kind=kOutput, calls=%fused_computation.100 | convolution fusion | flops 5033573888 | bytes 23236608 | tf_op jit(solution)/shard_map/dot_general | solution.py:130
  267.7 0.1 select_reduce_fusion.7
  267.9 0.2 select_reduce_fusion.6
  268.1 0.2 fusion.16
  268.3 0.2 select_reduce_fusion.5
  268.5 0.2 fusion.36
  268.7 0.3 select_reduce_fusion.4
  269.0 0.3 fusion.15
  269.3 0.3 select_reduce_fusion.3
  269.6 0.3 fusion.27
  269.9 0.4 select_reduce_fusion.2
  270.3 0.4 fusion.14
  270.7 0.4 select_reduce_fusion.1
  271.1 0.4 select_reduce_fusion
  271.6 1.2 concatenate.9
  272.9 4.0 %all-to-all-start.1 = ((f32[4,128,11]{1,2,0:T(8,128)}), f32[4,128,11]{1,2,0:T(8,128)S(1)}, u32[]{:S(2)}, u32[]{:S(2)}) async-start(f32[4,128,11]{1,2,0:T(8,128)} %concatenate.9), calls=%async_computation.1 | async-start | bytes 65536 | tf_op jit(solution)/shard_map/all_to_all | solution.py:136
  276.9 4.3 %all-to-all-done.1 = f32[4,128,11]{1,2,0:T(8,128)S(1)} async-done(((f32[4,128,11]{1,2,0:T(8,128)}), f32[4,128,11]{1,2,0:T(8,128)S(1)}, u32[]{:S(2)}, u32[]{:S(2)}) %all-to-all-start.1) | async-done | bytes 22560 | tf_op jit(solution)/shard_map/all_to_all | solution.py:136
  282.5 0.8 broadcast_in_dim.200
  283.3 8.0 %all-to-all-start.2 = ((f32[64,128,11]{1,2,0:T(8,128)}), f32[64,128,11]{1,2,0:T(8,128)S(1)}, u32[]{:S(2)}, u32[]{:S(2)}) async-start(f32[64,128,11]{1,2,0:T(8,128)} %broadcast_in_dim.200), calls=%async_computation.2 | async-start | bytes 1048576 | tf_op jit(solution)/shard_map/all_to_all | solution.py:138
  291.4 17.7 %all-to-all-done.2 = f32[64,128,11]{1,2,0:T(8,128)S(1)} async-done(((f32[64,128,11]{1,2,0:T(8,128)}), f32[64,128,11]{1,2,0:T(8,128)S(1)}, u32[]{:S(2)}, u32[]{:S(2)}) %all-to-all-start.2) | async-done | bytes 360480 | tf_op jit(solution)/shard_map/all_to_all | solution.py:138
  309.2 0.7 copy.32
  310.0 0.1 select_reduce_fusion.15
  310.1 0.2 fusion.26
  310.3 0.2 select_reduce_fusion.14
  310.4 0.2 fusion.19
  310.6 0.2 select_reduce_fusion.13
  310.7 0.2 fusion.35
  310.9 0.2 select_reduce_fusion.12
  311.1 0.2 fusion.20
  311.2 0.2 select_reduce_fusion.11
  311.4 0.2 fusion.31
  311.6 0.2 select_reduce_fusion.10
  311.8 0.2 fusion.21
  312.0 0.2 select_reduce_fusion.9
  312.2 0.2 select_reduce_fusion.8
  312.4 0.6 concatenate.11
  (35 shorter events, 1.8 us)
Async XLA Ops:
  7.2 219.4 %all-gather.2.cloned.1.call-start = ((), (), s32[]{:S(2)}) async-start(), calls=%async_computation.3 | async-start | bytes 12632064 | tf_op jit(solution)/shard_map/all_gather | solution.py:109
  7.2 100.6 %copy-start.2 = (s32[4,128]{1,0:T(4,128)S(1)}, s32[4,128]{1,0:T(4,128)}, u32[]{:S(2)}) copy-start(s32[4,128]{1,0:T(4,128)} %param.11) | copy-start | bytes 6148
  226.6 22.6 %copy-start = (bf16[49152,128]{1,0:T(8,128)(2,1)S(1)}, bf16[49152,128]{1,0:T(8,128)(2,1)}, u32[]{:S(2)}) copy-start(bf16[49152,128]{1,0:T(8,128)(2,1)} %all-gather.2.cloned.1.call-done) | copy-start | bytes 37748740
  226.6 23.4 %copy-start.1 = (bf16[4,12288,128]{2,1,0:T(8,128)(2,1)S(1)}, bf16[4,12288,128]{2,1,0:T(8,128)(2,1)}, u32[]{:S(2)}) copy-start(bf16[4,12288,128]{2,1,0:T(8,128)(2,1)} %copy.31) | copy-start | bytes 37748740
  272.9 8.3 %all-to-all-start.1 = ((f32[4,128,11]{1,2,0:T(8,128)}), f32[4,128,11]{1,2,0:T(8,128)S(1)}, u32[]{:S(2)}, u32[]{:S(2)}) async-start(f32[4,128,11]{1,2,0:T(8,128)} %concatenate.9), calls=%async_computation.1 | async-start | bytes 65536 | tf_op jit(solution)/shard_map/all_to_all | solution.py:136
  283.3 25.7 %all-to-all-start.2 = ((f32[64,128,11]{1,2,0:T(8,128)}), f32[64,128,11]{1,2,0:T(8,128)S(1)}, u32[]{:S(2)}, u32[]{:S(2)}) async-start(f32[64,128,11]{1,2,0:T(8,128)} %broadcast_in_dim.200), calls=%async_computation.2 | async-start | bytes 1048576 | tf_op jit(solution)/shard_map/all_to_all | solution.py:138
Sparse Core Ops, SparseCore 0:
  108.0 118.5 all-gather.1
